TPU v7x, 512 devices: a whole 4x4x16 slice. The times are simulated.
512 devices in a mesh: role: 4 (over y), dp: 8 (over x, core), tp: 16 (over z).
Axes of the slice: x: 4, y: 4, z: 16, core: 2. Of those that a mesh axis runs over, the one named last changes fastest.
Arguments:
- ref_logits: bfloat16 [4096, 77824], P(('role', 'dp'), 'tp'), may hold values from -30 to 250
- token_ids: int32 [4096], P(('role', 'dp')), may hold values from 0 to 77823
- old_logp: bfloat16 [4096], P(('role', 'dp')), may hold values from -28 to -4
- owner_of_row: int32 [4096], P(('role', 'dp')), may hold values from 0 to 31, as said below
- lengths: int32 [64], P(('role', 'dp')), may hold values from 1 to 64
- rewards: float32 [64], replicated, may hold values from 0 to 1
- group_ids: int32 [64], replicated, may hold values from 0 to 7
- pol_logits: bfloat16 [6144, 77824], P(('role', 'dp'), 'tp'), may hold values from -30 to 250
Outputs:
- grad_logits: bfloat16 [6144, 77824], P(('role', 'dp'), 'tp')
- token_loss: float32 [6144], P(('role', 'dp'))
Inputs may be any that keep to these rules, and one draw needn't show every extreme that they name: `owner_of_row`: among the rows of one owner (aligned blocks of 128 rows) at most 6 name the same owner; one owner drawn from the seed is named by exactly 6 rows in every block.
All inputs are finite; a program needn't handle non-finite values.
Results may differ from a plain program's by a relative error of at most 0.001.
Values may be sent and summed in bfloat16 or wider, within the bound.
No kernel may reach another device: no remote copies, remote signals or barrier semaphores. Data moves between devices by JAX's collectives and lax.ppermute only.
A program may use at most 64 MiB of HBM per device.

v0:
```python
import jax
import jax.numpy as jnp
from jax import lax
from jax.sharding import PartitionSpec as P

kl_weight = 0.04
low_bound = 0.8
high_bound = 1.2
dual_bound = 3.0
ratio_clamp = 20.0


def shards(ref_logits, token_ids, old_logp, owner_of_row, lengths, rewards, group_ids, pol_logits):
    role_count = lax.axis_size("role")
    data_count = lax.axis_size("dp")
    owner_count = role_count * data_count
    my_owner = lax.axis_index("role") * data_count + lax.axis_index("dp")
    row_count = ref_logits.shape[0]
    vocab_local = ref_logits.shape[1]
    slot_count = pol_logits.shape[0]
    capacity = slot_count // owner_count
    seq_count = rewards.shape[0]
    seq_local = lengths.shape[0]
    row_span = row_count // seq_local
    member = (group_ids[:, None] == jnp.arange(seq_count)[None, :]).astype(jnp.float32)
    group_total = jnp.sum(member * rewards[:, None], axis=0)
    group_count = jnp.sum(member, axis=0)
    group_mean = group_total / jnp.maximum(group_count, 1.0)
    advantage = rewards - jnp.sum(member * group_mean[None, :], axis=1)
    row_index = jnp.arange(row_count)
    row_valid = row_index % row_span < jnp.repeat(lengths, row_span)
    seq_tag = jnp.where(row_valid, my_owner * seq_local + row_index // row_span, -1)
    valid_total = lax.psum(jnp.sum(row_valid.astype(jnp.float32)), ("role", "dp"))
    owner_hot = (owner_of_row[:, None] == jnp.arange(owner_count)[None, :]).astype(jnp.int32)
    earlier = jnp.cumsum(owner_hot, axis=0) - owner_hot
    row_rank = jnp.sum(earlier * owner_hot, axis=1)
    send_slot = owner_of_row * capacity + row_rank
    picker = send_slot[None, :] == jnp.arange(slot_count)[:, None]
    sent_rows = jnp.dot(
        picker.astype(jnp.bfloat16), ref_logits, preferred_element_type=jnp.float32
    ).astype(jnp.bfloat16)
    sent_ids = jnp.sum(jnp.where(picker, token_ids[None, :], 0), axis=1)
    sent_tags = jnp.sum(jnp.where(picker, seq_tag[None, :] + 1, 0), axis=1) - 1
    sent_old = jnp.sum(
        jnp.where(picker, old_logp.astype(jnp.float32)[None, :], 0.0), axis=1
    ).astype(jnp.bfloat16)
    send_shape = (owner_count, capacity)
    arrived = (
        lax.all_to_all(
            sent_rows.reshape(send_shape + (vocab_local,)),
            ("role", "dp"),
            split_axis=0,
            concat_axis=0,
            tiled=True,
        ),
        lax.all_to_all(
            sent_ids.reshape(send_shape), ("role", "dp"), split_axis=0, concat_axis=0, tiled=True
        ),
        lax.all_to_all(
            sent_old.reshape(send_shape), ("role", "dp"), split_axis=0, concat_axis=0, tiled=True
        ),
        lax.all_to_all(
            sent_tags.reshape(send_shape), ("role", "dp"), split_axis=0, concat_axis=0, tiled=True
        ),
    )
    got_rows = arrived[0].reshape(slot_count, vocab_local)
    got_ids = arrived[1].reshape(slot_count)
    got_old = arrived[2].reshape(slot_count)
    got_tags = arrived[3].reshape(slot_count)
    policy = pol_logits.astype(jnp.float32)
    ref_rows = got_rows.astype(jnp.float32)
    column_base = lax.axis_index("tp") * vocab_local
    token_hit = jnp.arange(vocab_local)[None, :] == (got_ids - column_base)[:, None]
    local_logit = jnp.sum(jnp.where(token_hit, policy, 0.0), axis=1)
    peak_p, peak_q = lax.pmax((jnp.max(policy, axis=1), jnp.max(ref_rows, axis=1)), "tp")
    policy_exp = jnp.exp(policy - peak_p[:, None])
    total_p, cross_sum, token_logit, total_q = lax.psum(
        (
            jnp.sum(policy_exp, axis=1),
            jnp.sum(policy_exp * (policy - ref_rows), axis=1),
            local_logit,
            jnp.sum(jnp.exp(ref_rows - peak_q[:, None]), axis=1),
        ),
        "tp",
    )
    slot_valid = got_tags >= 0
    slot_adv = jnp.sum(
        jnp.where(got_tags[:, None] == jnp.arange(seq_count)[None, :], advantage[None, :], 0.0),
        axis=1,
    )
    loss_scale = row_count * owner_count / valid_total
    log_p = peak_p + jnp.log(total_p)
    log_q = peak_q + jnp.log(total_q)
    mean_gap = cross_sum / total_p
    kl_term = mean_gap - log_p + log_q
    raw_log_ratio = token_logit - log_p - got_old.astype(jnp.float32)
    prob_ratio = jnp.exp(jnp.clip(raw_log_ratio, -ratio_clamp, ratio_clamp))
    plain_loss = -slot_adv * prob_ratio
    clipped_loss = -slot_adv * jnp.clip(prob_ratio, low_bound, high_bound)
    upper_loss = jnp.maximum(plain_loss, clipped_loss)
    dual_loss = -dual_bound * slot_adv
    negative = slot_adv < 0.0
    policy_loss = jnp.where(negative, jnp.minimum(upper_loss, dual_loss), upper_loss)
    token_losses = jnp.where(slot_valid, policy_loss + kl_weight * kl_term, 0.0)
    inside = (prob_ratio > low_bound) & (prob_ratio < high_bound)
    token_coef = jnp.where((plain_loss >= clipped_loss) | inside, plain_loss, 0.0)
    token_coef = jnp.where(negative & (upper_loss > dual_loss), 0.0, token_coef)
    token_coef = jnp.where(jnp.abs(raw_log_ratio) < ratio_clamp, token_coef, 0.0)
    policy_prob = policy_exp / total_p[:, None]
    grad_rows = token_coef[:, None] * (token_hit.astype(jnp.float32) - policy_prob)
    grad_rows = grad_rows + kl_weight * policy_prob * (policy - ref_rows - mean_gap[:, None])
    grad_rows = jnp.where(slot_valid[:, None], loss_scale * grad_rows, 0.0).astype(jnp.bfloat16)
    return (grad_rows, token_losses)


def solution(mesh):
    return jax.shard_map(
        shards,
        mesh=mesh,
        in_specs=(
            P(("role", "dp"), "tp"),
            P(("role", "dp")),
            P(("role", "dp")),
            P(("role", "dp")),
            P(("role", "dp")),
            P(),
            P(),
            P(("role", "dp"), "tp"),
        ),
        out_specs=(P(("role", "dp"), "tp"), P(("role", "dp"))),
        check_vma=False,
    )
```

profile of v0, /device:TPU:32, one launch (start us, length us, event | category | flops | bytes accessed | tf_op | source)
XLA Modules:
  0.0 222.8 jit_solution(16577412321669968266)
XLA Ops:
  0.6 0.0 copy-start
  0.7 0.8 convert_element_type.58
  1.4 0.7 broadcast_in_dim.88
  2.1 0.1 reshape.130
  2.2 0.7 fusion.6
  3.0 0.2 reduce_window_sum.11
  3.1 0.8 select_reduce_fusion.4
  4.0 0.7 fusion.13
  4.6 0.1 select_reduce_fusion
  4.7 0.7 convert_element_type.72
  5.5 7.3 %all-to-all-start.2 = ((bf16[32,1,6]{2,1,0:T(2,128)(2,1)}), bf16[32,1,6]{2,1,0:T(2,128)(2,1)S(1)}, u32[]{:S(2)}, u32[]{:S(2)}) async-start(bf16[32,1,6]{2,1,0:T(2,128)(2,1)} %convert_element_type.72), calls=%async_computation.2 | async-start | bytes 32768 | tf_op jit(solution)/shard_map/all_to_all | solution.py:59
  12.8 0.8 select_reduce_fusion.1
  13.6 0.7 sub.77
  14.3 5.8 %all-to-all-done.2 = bf16[32,1,6]{2,1,0:T(2,128)(2,1)S(1)} async-done(((bf16[32,1,6]{2,1,0:T(2,128)(2,1)}), bf16[32,1,6]{2,1,0:T(2,128)(2,1)S(1)}, u32[]{:S(2)}, u32[]{:S(2)}) %all-to-all-start.2) | async-done | bytes 416 | tf_op jit(solution)/shard_map/all_to_all | solution.py:59
  20.1 3.8 %all-to-all-start = ((s32[32,1,6]{2,1,0:T(1,128)}), s32[32,1,6]{2,1,0:T(1,128)S(1)}, u32[]{:S(2)}, u32[]{:S(2)}) async-start(s32[32,1,6]{2,1,0:T(1,128)} %bitcast), calls=%async_computation | async-start | bytes 32768 | tf_op jit(solution)/shard_map/all_to_all | solution.py:62
  24.0 0.7 all_to_all.18
  24.7 6.6 %all-to-all-done = s32[32,1,6]{2,1,0:T(1,128)S(1)} async-done(((s32[32,1,6]{2,1,0:T(1,128)}), s32[32,1,6]{2,1,0:T(1,128)S(1)}, u32[]{:S(2)}, u32[]{:S(2)}) %all-to-all-start) | async-done | bytes 800 | tf_op jit(solution)/shard_map/all_to_all | solution.py:62
  31.3 3.8 %all-to-all-start.1 = ((s32[32,1,6]{2,1,0:T(1,128)}), s32[32,1,6]{2,1,0:T(1,128)S(1)}, u32[]{:S(2)}, u32[]{:S(2)}) async-start(s32[32,1,6]{2,1,0:T(1,128)} %bitcast.1), calls=%async_computation.1 | async-start | bytes 32768 | tf_op jit(solution)/shard_map/all_to_all | solution.py:56
  35.1 0.0 copy-done
  35.1 1.9 convolution_convert_fusion
  37.0 4.2 %reshape.132 = bf16[32,6,4864]{2,1,0:T(8,128)(2,1)} reshape(bf16[192,4864]{1,0:T(8,128)(2,1)} %convolution_convert_fusion) | data formatting | bytes 3735552 | tf_op jit(solution)/shard_map/reshape | solution.py:50
  41.2 1.3 all-to-all-done.1
  42.4 6.2 %all-to-all-start.3 = ((bf16[32,6,4864]{2,1,0:T(8,128)(2,1)}), bf16[32,6,4864]{2,1,0:T(8,128)(2,1)}, u32[]{:S(2)}, u32[]{:S(2)}) async-start(bf16[32,6,4864]{2,1,0:T(8,128)(2,1)} %reshape.132), calls=%async_computation.3 | async-start | bytes 4980736 | tf_op jit(solution)/shard_map/all_to_all | solution.py:49
  48.7 0.7 fusion.11
  49.4 87.7 %psum.35 = f32[]{:T(128)} all-reduce(f32[]{:T(128)} %fusion.11), channel_id=1, replica_groups=mesh['role'=4,'dp'=8,'tp'=16] {'role','dp'}, use_global_device_ids=true, to_apply=%region_4.5 | all-reduce | flops 1 | bytes 8 | tf_op jit(solution)/shard_map/psum | solution.py:33
  137.1 0.1 convert_reduce_fusion
  137.2 0.2 select_reduce_fusion.5
  138.1 0.0 copy-done.1
  138.1 0.3 reduce_max.30
  138.4 0.1 convert_reduce_fusion.1
  138.5 0.1 reshape.133
  138.6 0.5 broadcast.142
  139.1 0.7 reduce.16
  139.8 0.1 reshape.131
  140.0 0.1 sub.80
  140.1 0.1 select_reduce_fusion.3
  140.2 0.0 all-to-all-done.3
  140.2 2.3 %reduce_max.32 = bf16[32,6]{1,0:T(8,128)(2,1)S(1)} reduce(bf16[32,6,4864]{2,1,0:T(8,128)(2,1)} %all-to-all-done.3, bf16[]{:T(256)} %constant.86.clone.1), dimensions={2}, to_apply=%region_19.20 | reduce | flops 933696 | bytes 1868162 | tf_op jit(solution)/shard_map/reduce_max | solution.py:75
  142.5 0.1 reshape.135
  142.6 34.4 %all-reduce.1 = (f32[192]{0:T(256)S(1)}, f32[192]{0:T(256)S(1)}) all-reduce(bf16[192]{0:T(256)(128)(2,1)S(1)} %reduce_max.30, f32[192]{0:T(256)S(1)} %reshape.135), channel_id=1, replica_groups=mesh['role'=4,'dp'=8,'tp'=16] {'tp'}, use_global_device_ids=true, to_apply=%region_9.10 | all-reduce | flops 384 | bytes 2688 | tf_op jit(solution)/shard_map/pmax | solution.py:75
  177.0 0.1 sub.91
  177.1 2.8 %exponential_reduce_fusion = f32[32,6]{1,0:T(8,128)S(1)} fusion(f32[32,6]{1,0:T(8,128)S(1)} %sub.91, bf16[32,6,4864]{2,1,0:T(8,128)(2,1)} %all-to-all-done.3), kind=kLoop, calls=%fused_computation.4 | loop fusion | flops 2801472 | bytes 1869312 | tf_op jit(solution)/shard_map/reduce_sum | solution.py:82
  179.9 0.1 reduce_sum.132
  180.0 4.3 %reshape.134 = f32[192,4864]{1,0:T(8,128)} reshape(bf16[32,6,4864]{2,1,0:T(8,128)(2,1)} %all-to-all-done.3) | data formatting | bytes 5603328 | tf_op jit(solution)/shard_map/convert_element_type | solution.py:71
  184.3 3.6 %fusion.4 = (f32[192]{0:T(256)S(1)}, f32[192]{0:T(256)S(1)}, f32[192]{0:T(256)S(1)}) fusion(bf16[192,4864]{1,0:T(8,128)(2,1)S(1)} %copy-done.1, f32[192]{0:T(256)S(1)} %get-tuple-element.13, f32[192,4864]{1,0:T(8,128)} %reshape.134, s32[192]{0:T(256)S(1)} %sub.80), kind=kLoop, calls=%fused_computation.9 | loop fusion | flops 8404416 | bytes 5607168 | tf_op jit(solution)/shard_map/reduce_sum | solution.py:79
  188.0 29.2 %all-reduce = (f32[192]{0:T(256)S(1)}, f32[192]{0:T(256)S(1)}, f32[192]{0:T(256)S(1)}, f32[192]{0:T(256)S(1)}) all-reduce(f32[192]{0:T(256)S(1)} %get-tuple-element.3, f32[192]{0:T(256)S(1)} %get-tuple-element.2, f32[192]{0:T(256)S(1)} %get-tuple-element.4, f32[192]{0:T(256)S(1)} %reduce_sum.132), channel_id=1, replica_groups=mesh['role'=4,'dp'=8,'tp'=16] {'tp'}, use_global_device_ids=true, to_apply=%region_18.19 | all-reduce | flops 768 | bytes 6144 | tf_op jit(solution)/shard_map/psum | solution.py:77
  217.2 0.6 fusion.9
  217.8 5.0 %select_convert_fusion = bf16[192,4864]{1,0:T(8,128)(2,1)} fusion(bf16[192,4864]{1,0:T(8,128)(2,1)S(1)} %copy-done.1, f32[192,4864]{1,0:T(8,128)} %reshape.134, f32[192]{0:T(256)S(1)} %get-tuple-element.17, f32[192]{0:T(256)S(1)} %get-tuple-element.10, f32[192]{0:T(256)S(1)} %get-tuple-element.18, f32[192]{0:T(256)S(1)} %get-tuple-element.13, ...), kind=kLoop, calls=%fused_computation.11 | loop fusion | flops 14008320 | bytes 7475140 | tf_op jit(solution)/shard_map/convert_element_type | solution.py:112
  (11 shorter events, 0.1 us)
Async XLA Ops:
  0.6 34.5 %copy-start = (bf16[128,4864]{1,0:T(8,128)(2,1)S(1)}, bf16[128,4864]{1,0:T(8,128)(2,1)}, u32[]{:S(2)}) copy-start(bf16[128,4864]{1,0:T(8,128)(2,1)} %param.8) | copy-start | bytes 3735556
  5.5 14.7 %all-to-all-start.2 = ((bf16[32,1,6]{2,1,0:T(2,128)(2,1)}), bf16[32,1,6]{2,1,0:T(2,128)(2,1)S(1)}, u32[]{:S(2)}, u32[]{:S(2)}) async-start(bf16[32,1,6]{2,1,0:T(2,128)(2,1)} %convert_element_type.72), calls=%async_computation.2 | async-start | bytes 32768 | tf_op jit(solution)/shard_map/all_to_all | solution.py:59
  20.1 11.1 %all-to-all-start = ((s32[32,1,6]{2,1,0:T(1,128)}), s32[32,1,6]{2,1,0:T(1,128)S(1)}, u32[]{:S(2)}, u32[]{:S(2)}) async-start(s32[32,1,6]{2,1,0:T(1,128)} %bitcast), calls=%async_computation | async-start | bytes 32768 | tf_op jit(solution)/shard_map/all_to_all | solution.py:62
  31.3 11.2 %all-to-all-start.1 = ((s32[32,1,6]{2,1,0:T(1,128)}), s32[32,1,6]{2,1,0:T(1,128)S(1)}, u32[]{:S(2)}, u32[]{:S(2)}) async-start(s32[32,1,6]{2,1,0:T(1,128)} %bitcast.1), calls=%async_computation.1 | async-start | bytes 32768 | tf_op jit(solution)/shard_map/all_to_all | solution.py:56
  37.0 11.7 %copy-start.4 = (s32[2]{0:T(128)S(1)}, s32[2]{0:T(128)}, u32[]{:S(2)}) copy-start(s32[2]{0:T(128)} %param.12) | copy-start | bytes 28
  37.0 100.1 %copy-start.2 = (s32[64]{0:T(128)S(1)}, s32[64]{0:T(128)}, u32[]{:S(2)}) copy-start(s32[64]{0:T(128)} %param.14) | copy-start | bytes 772
  37.0 100.1 %copy-start.3 = (f32[64]{0:T(128)S(1)}, f32[64]{0:T(128)}, u32[]{:S(2)}) copy-start(f32[64]{0:T(128)} %param.13) | copy-start | bytes 772
  37.0 101.1 %copy-start.1 = (bf16[192,4864]{1,0:T(8,128)(2,1)S(1)}, bf16[192,4864]{1,0:T(8,128)(2,1)}, u32[]{:S(2)}) copy-start(bf16[192,4864]{1,0:T(8,128)(2,1)} %param.15) | copy-start | bytes 5603332
  42.4 97.7 %all-to-all-start.3 = ((bf16[32,6,4864]{2,1,0:T(8,128)(2,1)}), bf16[32,6,4864]{2,1,0:T(8,128)(2,1)}, u32[]{:S(2)}, u32[]{:S(2)}) async-start(bf16[32,6,4864]{2,1,0:T(8,128)(2,1)} %reshape.132), calls=%async_computation.3 | async-start | bytes 4980736 | tf_op jit(solution)/shard_map/all_to_all | solution.py:49
where the time goes:
time: 223 us
  blocking collectives  151 us (68%)
  starting transfers between devices  21.2 us (10%)
  other arithmetic  20.6 us (9%)
  waiting for transfers between devices  13.6 us (6%)
  local copies, waits for them, and re-layouts  12.6 us (6%)
    psum x1, blocking collectives, shards(): lax.psum(jnp.sum(row_valid.astype(jnp.float32)), ('role', 'dp'))  87.7 us
    pmax x1, blocking collectives, shards(): lax.pmax((jnp.max(policy, axis=1), jnp.max(ref_rows, axis=1)), 'tp')  34.4 us
    psum x1, blocking collectives, shards(): lax.psum((jnp.sum(policy_exp, axis=1), jnp.sum(policy_exp * (policy - ref...  29.2 us
    all_to_all x1, starting transfers between devices, shards(): lax.all_to_all(sent_old.reshape(send_shape), ('role', 'dp'), split_axis=0...  7.32 us
    all_to_all x1, waiting for transfers between devices, shards(): lax.all_to_all(sent_tags.reshape(send_shape), ('role', 'dp'), split_axis=...  6.57 us
    all_to_all x1, starting transfers between devices, shards(): lax.all_to_all(sent_rows.reshape(send_shape + (vocab_local,)), ('role', '...  6.24 us
    all_to_all x1, waiting for transfers between devices, shards(): lax.all_to_all(sent_old.reshape(send_shape), ('role', 'dp'), split_axis=0...  5.82 us
    convert_element_type x1, other arithmetic, shards(): jnp.where(slot_valid[:, None], loss_scale * grad_rows, 0.0)  4.99 us
  transfers between devices with their start and end apart: 4, of which 3 were waited for; matrix products, arithmetic and copies ran while one was open for 5% of the time, Pallas kernels for 0%

commit v1 on v0

v1 whole, which is shorter than its diff:
```python
import functools

import jax
import jax.numpy as jnp
from jax import lax
from jax.experimental import pallas as pl
from jax.experimental.pallas import tpu as pltpu
from jax.sharding import PartitionSpec as P

kl_weight = 0.04
low_bound = 0.8
high_bound = 1.2
dual_bound = 3.0
ratio_clamp = 20.0

LANES = 128
GROUP = 4
OCTET = 8
VMEM_LIMIT = 16 * 1024 * 1024

f32 = jnp.float32
bf16 = jnp.bfloat16
i32 = jnp.int32


def iota(shape, dim):
    return lax.broadcasted_iota(i32, shape, dim)


def send_kernel(cap, ids_ref, old_ref, owner_ref, len_ref, ref_ref, send_ref):
    rows = ref_ref.shape[0]
    blocks = ref_ref.shape[1] // LANES
    owners = send_ref.shape[0]
    groups = send_ref.shape[1] // (GROUP * cap)
    seq_local = len_ref.shape[0]
    span = rows // seq_local
    me = lax.axis_index("role") * lax.axis_size("dp") + lax.axis_index("dp")

    owner = owner_ref[...].reshape(1, rows)
    hot = (iota((owners, rows), 0) == owner).astype(f32)
    before = (iota((rows, rows), 0) < iota((rows, rows), 1)).astype(bf16)
    earlier = jnp.dot(hot.astype(bf16), before, preferred_element_type=f32)
    rank = jnp.sum(earlier * hot, axis=0, keepdims=True).astype(i32)
    slot = owner * cap + rank

    lane = iota((1, rows), 1)
    tag = jnp.zeros((1, rows), i32)
    count = jnp.int32(0)
    for s in range(seq_local):
        length = len_ref[s]
        inside = (lane >= s * span) & (lane < s * span + jnp.minimum(length, span))
        tag = jnp.where(inside, me * seq_local + s + 1, tag)
        count = count + jnp.clip(length, 0, span)
    ids = ids_ref[...].reshape(1, rows)
    feature = iota((LANES, rows), 0)
    table = jnp.zeros((LANES, rows), f32)
    values = (
        (ids & 255).astype(f32),
        ((ids >> 8) & 255).astype(f32),
        (ids >> 16).astype(f32),
        old_ref[...].reshape(1, rows).astype(f32),
        tag.astype(f32),
    )
    for n, value in enumerate(values):
        table = jnp.where(feature == n, value, table)
    table = table.T.astype(bf16)
    nothing = jnp.zeros((rows, LANES), bf16)

    def block(c):
        if c < blocks:
            return ref_ref[:, c * LANES : (c + 1) * LANES]
        return table if c == blocks else nothing

    tall = GROUP * cap
    row = iota((OCTET, tall, rows), 1)
    place = iota((OCTET, tall, rows), 0) * cap + row
    pickers = []
    for o in range(owners // OCTET):
        parts = []
        for c in range(GROUP):
            mine = (row >= c * cap) & (row < (c + 1) * cap)
            hit = mine & (place + o * OCTET * cap == slot.reshape(1, 1, rows) + c * cap)
            parts.append(hit.astype(f32).reshape(OCTET * tall, rows).astype(bf16))
        pickers.append(jnp.concatenate(parts, axis=1))
    last_row = iota((OCTET, tall, LANES), 1)
    for g in range(0, groups, 2):
        right = jnp.concatenate(
            [
                jnp.concatenate([block((g + h) * GROUP + c) for h in range(2)], axis=1)
                for c in range(GROUP)
            ],
            axis=0,
        )
        for o in range(owners // OCTET):
            out = jnp.dot(pickers[o], right, preferred_element_type=f32)
            for h in range(2):
                part = out[:, h * LANES : (h + 1) * LANES].reshape(OCTET, tall, LANES)
                if (g + h + 1) * GROUP > blocks + 1:
                    first = (blocks + 1 - (g + h) * GROUP) * cap
                    part = jnp.where(last_row >= first, count.astype(f32), part)
                send_ref[
                    o * OCTET : (o + 1) * OCTET, (g + h) * tall : (g + h + 1) * tall, :
                ] = part.astype(bf16)


def policy_kernel(pol_ref, exp_ref, stat_ref):
    slots, columns = pol_ref.shape
    step = 48
    lane = iota((step, LANES), 1)

    def body(i, carry):
        at = pl.ds(pl.multiple_of(i * step, 16), step)
        top = pol_ref[at, 0:LANES].astype(f32)
        for c in range(1, columns // LANES):
            top = jnp.maximum(top, pol_ref[at, c * LANES : (c + 1) * LANES].astype(f32))
        top = jnp.max(top, axis=1, keepdims=True)
        total = jnp.zeros((step, LANES), f32)
        for c in range(columns // LANES):
            part = jnp.exp(pol_ref[at, c * LANES : (c + 1) * LANES].astype(f32) - top)
            exp_ref[at, c * LANES : (c + 1) * LANES] = part
            total = total + part
        total = jnp.sum(total, axis=1, keepdims=True)
        stat_ref[at, :] = jnp.where(lane == 0, top, jnp.where(lane == 1, total, 0.0))
        return carry

    lax.fori_loop(0, slots // step, body, 0)


def partial_kernel(cap, got_ref, pol_ref, exp_ref, stat_ref, rows_ref, part_ref, meta_ref, column_ref):
    slots, columns = pol_ref.shape
    blocks = columns // LANES
    owners = got_ref.shape[0]
    tall = GROUP * cap
    wide = OCTET * cap
    groups = got_ref.shape[1] // tall
    base = lax.axis_index("tp") * columns

    size = OCTET * tall
    a = iota((GROUP, wide, size), 0)
    b = iota((GROUP, wide, size), 1)
    target = b + cap * a
    for d in range(1, OCTET):
        target = target + jnp.where(b >= d * cap, tall - cap, 0)
    order = (target == iota((GROUP, wide, size), 2)).astype(f32).reshape(size, size).astype(bf16)
    lane = iota((wide, LANES), 1)

    def body(o, carry):
        at = pl.ds(pl.multiple_of(o * wide, 16), wide)
        from_owner = pl.ds(o * OCTET, OCTET)

        def arrived(g):
            pair = [
                got_ref[from_owner, (g + h) * tall : (g + h + 1) * tall, :]
                .astype(f32)
                .reshape(size, LANES)
                .astype(bf16)
                for h in range(2)
            ]
            return jnp.dot(order, jnp.concatenate(pair, axis=1), preferred_element_type=f32)

        token = None
        top = jnp.full((wide, LANES), -jnp.inf, f32)
        cross = jnp.zeros((wide, LANES), f32)
        picked = jnp.zeros((wide, LANES), f32)
        info = counts = None
        for g in range(groups - 2, -1, -2):
            product = arrived(g)
            pieces = {
                (g + h) * GROUP + c: product[c * wide : (c + 1) * wide, h * LANES : (h + 1) * LANES]
                for h in range(2)
                for c in range(GROUP)
            }
            if blocks in pieces:
                info, counts = pieces[blocks], pieces[blocks + 1]
                token = (info[:, 0:1] + 256.0 * info[:, 1:2] + 65536.0 * info[:, 2:3]).astype(i32) - base
            for c in sorted(n for n in pieces if n < blocks):
                q = pieces[c]
                span = slice(c * LANES, (c + 1) * LANES)
                z = pol_ref[at, span].astype(f32)
                rows_ref[at, span] = q.astype(bf16)
                top = jnp.maximum(top, q)
                cross = cross + exp_ref[at, span] * (z - q)
                picked = picked + jnp.where(lane == token - c * LANES, z, 0.0)
        top = jnp.max(top, axis=1, keepdims=True)
        total = jnp.zeros((wide, LANES), f32)
        for c in range(blocks):
            total = total + jnp.exp(rows_ref[at, c * LANES : (c + 1) * LANES].astype(f32) - top)
        sums = (
            jnp.sum(cross, axis=1, keepdims=True),
            jnp.sum(picked, axis=1, keepdims=True),
            top,
            jnp.sum(total, axis=1, keepdims=True),
        )
        out = jnp.where(lane < 2, stat_ref[at, :], 0.0)
        for n, value in enumerate(sums):
            out = jnp.where(lane == 2 + n, value, out)
        for n, value in enumerate((info[:, 3:4], info[:, 4:5], token.astype(f32), counts[:, 0:1])):
            out = jnp.where(lane == 8 + n, value, out)
        column_ref[at, :] = out
        return carry

    lax.fori_loop(0, owners // OCTET, body, 0)
    column_ref[slots:, :] = jnp.zeros((column_ref.shape[0] - slots, LANES), f32)
    turned = column_ref[...].T
    part_ref[...] = jnp.broadcast_to(turned[None, 0:8, :], part_ref.shape)
    meta_ref[...] = turned[8:16, :]


def grad_kernel(cap, row_total, all_ref, mine_ref, meta_ref, rewards_ref, group_ref, pol_ref, rows_ref, exp_ref, grad_ref, loss_ref, turn_ref, column_ref):
    slots, columns = pol_ref.shape
    blocks = columns // LANES
    seqs = rewards_ref.shape[0]
    wide = OCTET * cap
    padded = meta_ref.shape[1]

    rewards = rewards_ref[...].reshape(1, seqs)
    groups = group_ref[...].reshape(1, seqs)
    diagonal = iota((seqs, seqs), 0) == iota((seqs, seqs), 1)
    group_down = jnp.sum(jnp.where(diagonal, groups, 0), axis=1, keepdims=True)
    reward_down = jnp.sum(jnp.where(diagonal, rewards, 0.0), axis=1, keepdims=True)
    same = (group_down == groups).astype(f32)
    mean = jnp.sum(same * rewards, axis=1, keepdims=True) / jnp.sum(same, axis=1, keepdims=True)
    advantage = reward_down - mean

    old, tag, token, counts = (meta_ref[n : n + 1, :] for n in range(4))
    valid = tag > 0.5
    adv = jnp.sum(
        jnp.where(iota((seqs, padded), 0) + 1 == tag.astype(i32), advantage, 0.0), axis=0, keepdims=True
    )
    valid_total = jnp.sum(jnp.where(iota((1, padded), 1) < slots, counts, 0.0)) / cap

    peaks, totals, crosses, tokens, peaks_q, totals_q = (all_ref[:, n, :] for n in range(6))
    peak = jnp.max(peaks, axis=0, keepdims=True)
    shift = jnp.exp(peaks - peak)
    total = jnp.sum(totals * shift, axis=0, keepdims=True)
    gap = jnp.sum(crosses * shift, axis=0, keepdims=True) / total
    peak_q = jnp.max(peaks_q, axis=0, keepdims=True)
    total_q = jnp.sum(totals_q * jnp.exp(peaks_q - peak_q), axis=0, keepdims=True)
    log_p = peak + jnp.log(total)
    log_q = peak_q + jnp.log(total_q)
    kl_term = gap - log_p + log_q
    raw = jnp.sum(tokens, axis=0, keepdims=True) - log_p - old
    ratio = jnp.exp(jnp.clip(raw, -ratio_clamp, ratio_clamp))
    plain = -adv * ratio
    clipped = -adv * jnp.clip(ratio, low_bound, high_bound)
    upper = jnp.maximum(plain, clipped)
    dual = -dual_bound * adv
    negative = adv < 0.0
    loss = jnp.where(negative, jnp.minimum(upper, dual), upper)
    loss_ref[...] = jnp.where(valid, loss + kl_weight * kl_term, 0.0)[:, :slots].reshape(slots)
    inside = (ratio > low_bound) & (ratio < high_bound)
    coef = jnp.where((plain >= clipped) | inside, plain, 0.0)
    coef = jnp.where(negative & (upper > dual), 0.0, coef)
    coef = jnp.where(jnp.abs(raw) < ratio_clamp, coef, 0.0)
    scale = jnp.where(valid, row_total / valid_total, 0.0)
    factor = scale * (jnp.exp(mine_ref[0, 0:1, :] - peak) / total)
    turn_ref[...] = jnp.zeros(turn_ref.shape, f32)
    for n, value in enumerate((factor * kl_weight, factor * coef, scale * coef, gap, token)):
        turn_ref[n : n + 1, :] = value
    column_ref[...] = turn_ref[...].T
    lane = iota((wide, LANES), 1)

    def body(o, carry):
        at = pl.ds(pl.multiple_of(o * wide, 16), wide)
        slope, level, spike, gaps, col = (
            jnp.broadcast_to(column_ref[at, n : n + 1], (wide, LANES)) for n in range(5)
        )
        where = col.astype(i32)
        for c in range(blocks):
            span = slice(c * LANES, (c + 1) * LANES)
            z = pol_ref[at, span].astype(f32)
            q = rows_ref[at, span].astype(f32)
            out = exp_ref[at, span] * (slope * ((z - q) - gaps) - level)
            out = out + jnp.where(lane == where - c * LANES, spike, 0.0)
            grad_ref[at, span] = out.astype(bf16)
        return carry

    lax.fori_loop(0, slots // wide, body, 0)


def call(kernel, out_shape, n_in, scratch=(), smem=(), cost=None):
    vmem = pl.BlockSpec(memory_space=pltpu.VMEM)
    scalar = pl.BlockSpec(memory_space=pltpu.SMEM)
    return pl.pallas_call(
        kernel,
        out_shape=out_shape,
        in_specs=[scalar if n in smem else vmem for n in range(n_in)],
        out_specs=jax.tree.map(lambda _: vmem, out_shape),
        scratch_shapes=list(scratch),
        compiler_params=pltpu.CompilerParams(vmem_limit_bytes=VMEM_LIMIT),
        cost_estimate=cost,
    )


def shards(ref_logits, token_ids, old_logp, owner_of_row, lengths, rewards, group_ids, pol_logits):
    owners = lax.axis_size("role") * lax.axis_size("dp")
    peers = lax.axis_size("tp")
    rows, columns = ref_logits.shape
    slots = pol_logits.shape[0]
    cap = slots // owners
    blocks = columns // LANES
    groups = -(-(blocks + 2) // (2 * GROUP)) * 2
    deep = groups * GROUP * cap
    padded = -(-slots // LANES) * LANES
    shape = jax.ShapeDtypeStruct
    everyone = ("role", "dp")

    send = call(
        functools.partial(send_kernel, cap), shape((owners, deep, LANES), bf16), 5, smem=(3,)
    )(token_ids, old_logp, owner_of_row, lengths, ref_logits)
    got = lax.all_to_all(send, everyone, split_axis=0, concat_axis=0, tiled=True)
    exps, stats = call(
        policy_kernel,
        (shape((slots, columns), f32), shape((slots, LANES), f32)),
        1,
        cost=pl.CostEstimate(
            flops=8 * slots * columns, bytes_accessed=6 * slots * columns, transcendentals=slots * columns
        ),
    )(pol_logits)
    got_rows, parts, meta = call(
        functools.partial(partial_kernel, cap),
        (shape((slots, columns), bf16), shape((peers, 8, padded), f32), shape((8, padded), f32)),
        4,
        scratch=(pltpu.VMEM((padded, LANES), f32),),
    )(got, pol_logits, exps, stats)
    everything = lax.all_to_all(parts, "tp", split_axis=0, concat_axis=0, tiled=True)
    return call(
        functools.partial(grad_kernel, cap, float(rows * owners)),
        (shape((slots, columns), bf16), shape((slots,), f32)),
        8,
        scratch=(pltpu.VMEM((LANES, padded), f32), pltpu.VMEM((padded, LANES), f32)),
    )(everything, parts, meta, rewards, group_ids, pol_logits, got_rows, exps)


def solution(mesh):
    return jax.shard_map(
        shards,
        mesh=mesh,
        in_specs=(
            P(("role", "dp"), "tp"),
            P(("role", "dp")),
            P(("role", "dp")),
            P(("role", "dp")),
            P(("role", "dp")),
            P(),
            P(),
            P(("role", "dp"), "tp"),
        ),
        out_specs=(P(("role", "dp"), "tp"), P(("role", "dp"))),
        check_vma=False,
    )
```

time: 223 us -> 82.2 us (0.37)
  blocking collectives: 151 us -> 27.5 us
  other arithmetic: 20.6 us -> 0 us
  starting transfers between devices: 21.2 us -> 7.57 us
  Pallas kernels: 0 us -> 11.9 us
  waiting for transfers between devices: 13.6 us -> 25.1 us
  local copies, waits for them, and re-layouts: 12.6 us -> 9.05 us
    psum x2 -> x0, blocking collectives: 117 us -> none  [the longest x1 87.7 us: shards(): lax.psum(jnp.sum(row_valid.astype(jnp.float32)), ('role', 'dp'))]
    pmax x1 -> x0, blocking collectives: 34.4 us -> none  [shards(): lax.pmax((jnp.max(policy, axis=1), jnp.max(ref_rows, axis=1)), 'tp')]
    all_to_all x0 -> x1, blocking collectives: none -> 27.5 us  [shards(): lax.all_to_all(parts, 'tp', split_axis=0, concat_axis=0, tiled=True)]
    all_to_all x4 -> x1, starting transfers between devices: 21.2 us -> 7.57 us  [shards(): lax.all_to_all(send, everyone, split_axis=0, concat_axis=0, tiled=True)]
    pallas_call x0 -> x4, Pallas kernels: none -> 11.9 us  [the longest x1 5.37 us: shards(): call(functools.partial(partial_kernel, cap), (shape((slots, columns), bf1...]
    all_to_all x4 -> x1, waiting for transfers between devices: 13.6 us -> 25.1 us  [shards(): lax.all_to_all(send, everyone, split_axis=0, concat_axis=0, tiled=True)]
    reduce_sum x9 -> x0, other arithmetic: 9.25 us -> none  [the longest x1 3.64 us: shards(): jnp.sum(policy_exp, axis=1)]
    unnamed x10 -> x22, local copies, waits for them, and re-layouts: 0.02 us -> 9.05 us
  transfers between devices with their start and end apart: 4 -> 1, of which waited for: 3 -> 1; matrix products, arithmetic and copies ran while one was open for 5% -> 0% of each run, Pallas kernels for 0% -> 2%
where the time goes in v1:
time: 82.2 us; the launch traced here: 81.9 us
  blocking collectives  27.5 us (33%)
  waiting for transfers between devices  25.1 us (31%)
  Pallas kernels  11.9 us (14%)
  local copies, waits for them, and re-layouts  9.05 us (11%)
  starting transfers between devices  7.57 us (9%)
    all_to_all x1, blocking collectives, shards(): lax.all_to_all(parts, 'tp', split_axis=0, concat_axis=0, tiled=True)  27.5 us
    all_to_all x1, waiting for transfers between devices, shards(): lax.all_to_all(send, everyone, split_axis=0, concat_axis=0, tiled=True)  25.1 us
    unnamed x22, local copies, waits for them, and re-layouts  9.05 us
    all_to_all x1, starting transfers between devices, shards(): lax.all_to_all(send, everyone, split_axis=0, concat_axis=0, tiled=True)  7.57 us
    pallas_call x1, Pallas kernels, shards(): call(functools.partial(partial_kernel, cap), (shape((slots, columns), bf1...  5.37 us
    pallas_call x1, Pallas kernels, shards(): call(functools.partial(grad_kernel, cap, float(rows * owners)), (shape((s...  3.22 us
    pallas_call x1, Pallas kernels, shards(): call(functools.partial(send_kernel, cap), shape((owners, deep, LANES), bf...  1.87 us
  transfers between devices with their start and end apart: 1, of which 1 were waited for; matrix products, arithmetic and copies ran while one was open for 0% of the time, Pallas kernels for 2%

profile of v1, /device:TPU:32, one launch (start us, length us, event | category | flops | bytes accessed | tf_op | source)
XLA Modules:
  0.0 81.9 jit_solution(9910335669980760463)
XLA Ops:
  0.6 0.0 copy-start.4
  0.6 1.3 %copy-done.4 = bf16[128,4864]{1,0:T(8,128)(2,1)S(1)} copy-done((bf16[128,4864]{1,0:T(8,128)(2,1)S(1)}, bf16[128,4864]{1,0:T(8,128)(2,1)}, u32[]{:S(2)}) %copy-start.4) | copy-done | bytes 1245208
  1.9 0.0 copy-start.7
  1.9 0.7 copy-done.7
  2.6 0.0 copy-start.8
  2.6 0.7 copy-done.8
  3.2 0.0 copy-start.9
  3.2 0.7 copy-done.9
  3.9 0.0 copy-start.10
  3.9 0.7 copy-done.10
  4.5 1.9 %shard_map.95 = bf16[32,240,128]{2,1,0:T(8,128)(2,1)S(1)} custom-call(s32[128]{0:T(128)S(1)} %copy-done.7, bf16[128]{0:T(256)(128)(2,1)S(1)} %copy-done.8, s32[128]{0:T(128)S(1)} %copy-done.9, s32[2]{0:T(128)S(1)} %copy-done.10, bf16[128,4864]{1,0:T(8,128)(2,1)S(1)} %copy-done.4), custom_call_target="tpu_custom_call" | custom-call | tf_op jit(solution)/shard_map/pallas_call | solution.py:308
  6.4 0.0 copy-start.3
  6.4 1.3 %copy-done.3 = bf16[32,240,128]{2,1,0:T(8,128)(2,1)} copy-done((bf16[32,240,128]{2,1,0:T(8,128)(2,1)}, bf16[32,240,128]{2,1,0:T(8,128)(2,1)S(1)}, u32[]{:S(2)}) %copy-start.3) | copy-done | bytes 1966104
  7.7 0.0 copy-start
  7.7 7.6 %all-to-all-start = ((bf16[32,240,128]{2,1,0:T(8,128)(2,1)}), bf16[32,240,128]{2,1,0:T(8,128)(2,1)}, u32[]{:S(2)}, u32[]{:S(2)}) async-start(bf16[32,240,128]{2,1,0:T(8,128)(2,1)} %copy-done.3), calls=%async_computation | async-start | bytes 3932160 | tf_op jit(solution)/shard_map/all_to_all | solution.py:311
  15.3 0.0 copy-done
  15.3 1.5 %shard_map.96 = (f32[192,4864]{1,0:T(8,128)S(1)}, f32[192,128]{1,0:T(8,128)S(1)}) custom-call(bf16[192,4864]{1,0:T(8,128)(2,1)S(1)} %copy-done), custom_call_target="tpu_custom_call" | custom-call | flops 7471104 | bytes 5603328 | tf_op jit(solution)/shard_map/pallas_call | solution.py:312
  16.8 0.0 copy-start.1
  16.8 1.8 %copy-done.1 = f32[192,4864]{1,0:T(8,128)} copy-done((f32[192,4864]{1,0:T(8,128)}, f32[192,4864]{1,0:T(8,128)S(1)}, u32[]{:S(2)}) %copy-start.1) | copy-done | bytes 3735576
  18.6 25.1 %all-to-all-done.got_ref = bf16[32,240,128]{2,1,0:T(8,128)(2,1)} async-done(((bf16[32,240,128]{2,1,0:T(8,128)(2,1)}), bf16[32,240,128]{2,1,0:T(8,128)(2,1)}, u32[]{:S(2)}, u32[]{:S(2)}) %all-to-all-start) | async-done | bytes 1966112 | tf_op jit(solution)/shard_map/all_to_all | solution.py:311
  43.7 0.0 copy-start.2
  43.7 2.1 %copy-done.2 = f32[192,4864]{1,0:T(8,128)S(1)} copy-done((f32[192,4864]{1,0:T(8,128)S(1)}, f32[192,4864]{1,0:T(8,128)}, u32[]{:S(2)}) %copy-start.2) | copy-done | bytes 3735576
  45.8 0.0 copy-start.5
  45.8 0.0 copy-start.6
  45.8 5.4 %shard_map.97 = (bf16[192,4864]{1,0:T(8,128)(2,1)S(1)}, f32[16,8,256]{2,1,0:T(8,128)S(1)}, f32[8,256]{1,0:T(8,128)S(1)}) custom-call(bf16[32,240,128]{2,1,0:T(8,128)(2,1)} %all-to-all-done.got_ref, bf16[192,4864]{1,0:T(8,128)(2,1)S(1)} %copy-done, f32[192,4864]{1,0:T(8,128)S(1)} %copy-done.2, f32[192,128]{1,0:T(8,128)S(1)} %get-tuple-element.8.stat_ref), custom_call_target="tpu_custom_call" | custom-call | tf_op jit(solution)/shard_map/pallas_call | solution.py:320
  51.1 27.5 %all_to_all.10.all_ref = f32[16,8,256]{2,1,0:T(8,128)S(1)} all-to-all(f32[16,8,256]{2,1,0:T(8,128)S(1)} %get-tuple-element.9.mine_ref), channel_id=1, replica_groups=mesh['role'=4,'dp'=8,'tp'=16] {'tp'}, dimensions={0} | all-to-all | bytes 262144 | tf_op jit(solution)/shard_map/all_to_all | solution.py:326
  78.6 0.0 copy-done.5
  78.6 0.0 copy-done.6
  78.7 3.2 %shard_map.98 = (bf16[192,4864]{1,0:T(8,128)(2,1)}, f32[192]{0:T(256)}) custom-call(f32[16,8,256]{2,1,0:T(8,128)S(1)} %all_to_all.10.all_ref, f32[16,8,256]{2,1,0:T(8,128)S(1)} %get-tuple-element.9.mine_ref, f32[8,256]{1,0:T(8,128)S(1)} %get-tuple-element.10.meta_ref, f32[64]{0:T(128)S(1)} %copy-done.5, s32[64]{0:T(128)S(1)} %copy-done.6, ...), custom_call_target="tpu_custom_call" | custom-call | tf_op jit(solution)/shard_map/pallas_call | solution.py:327
Async XLA Ops:
  0.6 1.3 %copy-start.4 = (bf16[128,4864]{1,0:T(8,128)(2,1)S(1)}, bf16[128,4864]{1,0:T(8,128)(2,1)}, u32[]{:S(2)}) copy-start(bf16[128,4864]{1,0:T(8,128)(2,1)} %ref_ref.1) | copy-start | bytes 3735556
  1.9 0.7 copy-start.7
  2.6 0.7 copy-start.8
  3.2 0.7 copy-start.9
  3.9 0.7 copy-start.10
  6.4 1.3 %copy-start.3 = (bf16[32,240,128]{2,1,0:T(8,128)(2,1)}, bf16[32,240,128]{2,1,0:T(8,128)(2,1)S(1)}, u32[]{:S(2)}) copy-start(bf16[32,240,128]{2,1,0:T(8,128)(2,1)S(1)} %shard_map.95) | copy-start | bytes 5898244
  7.7 7.6 %copy-start = (bf16[192,4864]{1,0:T(8,128)(2,1)S(1)}, bf16[192,4864]{1,0:T(8,128)(2,1)}, u32[]{:S(2)}) copy-start(bf16[192,4864]{1,0:T(8,128)(2,1)} %pol_ref.5) | copy-start | bytes 5603332
  7.7 36.0 %all-to-all-start = ((bf16[32,240,128]{2,1,0:T(8,128)(2,1)}), bf16[32,240,128]{2,1,0:T(8,128)(2,1)}, u32[]{:S(2)}, u32[]{:S(2)}) async-start(bf16[32,240,128]{2,1,0:T(8,128)(2,1)} %copy-done.3), calls=%async_computation | async-start | bytes 3932160 | tf_op jit(solution)/shard_map/all_to_all | solution.py:311
  16.8 1.8 %copy-start.1 = (f32[192,4864]{1,0:T(8,128)}, f32[192,4864]{1,0:T(8,128)S(1)}, u32[]{:S(2)}) copy-start(f32[192,4864]{1,0:T(8,128)S(1)} %get-tuple-element.7.exp_ref) | copy-start | bytes 11206660
  43.7 2.1 %copy-start.2 = (f32[192,4864]{1,0:T(8,128)S(1)}, f32[192,4864]{1,0:T(8,128)}, u32[]{:S(2)}) copy-start(f32[192,4864]{1,0:T(8,128)} %copy-done.1) | copy-start | bytes 11206660
  45.8 32.9 %copy-start.5 = (f32[64]{0:T(128)S(1)}, f32[64]{0:T(128)}, u32[]{:S(2)}) copy-start(f32[64]{0:T(128)} %rewards_ref.1) | copy-start | bytes 772
  45.8 32.9 %copy-start.6 = (s32[64]{0:T(128)S(1)}, s32[64]{0:T(128)}, u32[]{:S(2)}) copy-start(s32[64]{0:T(128)} %group_ref.1) | copy-start | bytes 772

commit v2 on v1

v2 whole, which is shorter than its diff:
```python
import functools

import jax
import jax.numpy as jnp
from jax import lax
from jax.experimental import pallas as pl
from jax.experimental.pallas import tpu as pltpu
from jax.sharding import PartitionSpec as P

kl_weight = 0.04
low_bound = 0.8
high_bound = 1.2
dual_bound = 3.0
ratio_clamp = 20.0

LANES = 128
GROUP = 4
OCTET = 8
VMEM_LIMIT = 16 * 1024 * 1024
WHOLE_VMEM = 60 * 1024 * 1024

f32 = jnp.float32
bf16 = jnp.bfloat16
i32 = jnp.int32


def iota(shape, dim):
    return lax.broadcasted_iota(i32, shape, dim)


def send_kernel(
    cap, ids_hbm, old_hbm, owner_hbm, len_hbm, ref_hbm, send_hbm, ids_ref, old_ref, owner_ref, len_ref, ref_ref, send_ref, small, load, store
):
    rows = ref_ref.shape[0]
    blocks = ref_ref.shape[1] // LANES
    owners = send_ref.shape[0]
    tall = GROUP * cap
    groups = send_ref.shape[1] // tall
    seq_local = len_ref.shape[0]
    span = rows // seq_local
    me = lax.axis_index("role") * lax.axis_size("dp") + lax.axis_index("dp")

    smalls = [
        pltpu.make_async_copy(source, target, small.at[n])
        for n, (source, target) in enumerate(
            ((owner_hbm, owner_ref), (ids_hbm, ids_ref), (old_hbm, old_ref), (len_hbm, len_ref))
        )
    ]
    loads = []
    for n, g in enumerate(range(0, groups, 2)):
        part = slice(g * GROUP * LANES, min((g + 2) * GROUP, blocks) * LANES)
        loads.append(pltpu.make_async_copy(ref_hbm.at[:, part], ref_ref.at[:, part], load.at[n]))
    for copy in smalls + loads:
        copy.start()

    before = (iota((rows, rows), 0) < iota((rows, rows), 1)).astype(bf16)
    lane = iota((1, rows), 1)
    feature = iota((LANES, rows), 0)
    smalls[0].wait()
    owner = owner_ref[...].reshape(1, rows)
    hot = (iota((owners, rows), 0) == owner).astype(f32)
    earlier = jnp.dot(hot.astype(bf16), before, preferred_element_type=f32)
    rank = jnp.sum(earlier * hot, axis=0, keepdims=True).astype(i32)
    slot = owner * cap + rank

    for copy in smalls[1:]:
        copy.wait()
    tag = jnp.zeros((1, rows), i32)
    count = jnp.int32(0)
    for s in range(seq_local):
        length = len_ref[s]
        inside = (lane >= s * span) & (lane < s * span + jnp.minimum(length, span))
        tag = jnp.where(inside, me * seq_local + s + 1, tag)
        count = count + jnp.clip(length, 0, span)
    ids = ids_ref[...].reshape(1, rows)
    table = jnp.zeros((LANES, rows), f32)
    values = (
        (ids & 255).astype(f32),
        ((ids >> 8) & 255).astype(f32),
        (ids >> 16).astype(f32),
        old_ref[...].reshape(1, rows).astype(f32),
        tag.astype(f32),
    )
    for n, value in enumerate(values):
        table = jnp.where(feature == n, value, table)
    table = table.T.astype(bf16)
    nothing = jnp.zeros((rows, LANES), bf16)

    def block(c):
        if c < blocks:
            return ref_ref[:, c * LANES : (c + 1) * LANES]
        return table if c == blocks else nothing

    row = iota((OCTET, tall, rows), 1)
    place = iota((OCTET, tall, rows), 0) * cap + row
    pickers = []
    for o in range(owners // OCTET):
        parts = []
        for c in range(GROUP):
            mine = (row >= c * cap) & (row < (c + 1) * cap)
            hit = mine & (place + o * OCTET * cap == slot.reshape(1, 1, rows) + c * cap)
            parts.append(hit.astype(f32).reshape(OCTET * tall, rows).astype(bf16))
        pickers.append(jnp.concatenate(parts, axis=1))
    last_row = iota((OCTET, tall, LANES), 1)
    stores = []
    for n, g in enumerate(range(0, groups, 2)):
        loads[n].wait()
        right = jnp.concatenate(
            [
                jnp.concatenate([block((g + h) * GROUP + c) for h in range(2)], axis=1)
                for c in range(GROUP)
            ],
            axis=0,
        )
        for o in range(owners // OCTET):
            out = jnp.dot(pickers[o], right, preferred_element_type=f32)
            for h in range(2):
                part = out[:, h * LANES : (h + 1) * LANES].reshape(OCTET, tall, LANES)
                if (g + h + 1) * GROUP > blocks + 1:
                    first = (blocks + 1 - (g + h) * GROUP) * cap
                    part = jnp.where(last_row >= first, count.astype(f32), part)
                send_ref[
                    o * OCTET : (o + 1) * OCTET, (g + h) * tall : (g + h + 1) * tall, :
                ] = part.astype(bf16)
        part = pl.ds(g * tall, 2 * tall)
        stores.append(pltpu.make_async_copy(send_ref.at[:, part, :], send_hbm.at[:, part, :], store.at[n]))
        stores[-1].start()
    for copy in stores:
        copy.wait()


def policy_kernel(pol_ref, stat_ref):
    slots, columns = pol_ref.shape
    step = 48
    lane = iota((step, LANES), 1)

    def body(i, carry):
        at = pl.ds(pl.multiple_of(i * step, 16), step)
        top = pol_ref[at, 0:LANES].astype(f32)
        for c in range(1, columns // LANES):
            top = jnp.maximum(top, pol_ref[at, c * LANES : (c + 1) * LANES].astype(f32))
        top = jnp.max(top, axis=1, keepdims=True)
        total = jnp.zeros((step, LANES), f32)
        for c in range(columns // LANES):
            total = total + jnp.exp(pol_ref[at, c * LANES : (c + 1) * LANES].astype(f32) - top)
        total = jnp.sum(total, axis=1, keepdims=True)
        stat_ref[at, :] = jnp.where(lane == 0, top, jnp.where(lane == 1, total, 0.0))
        return carry

    lax.fori_loop(0, slots // step, body, 0)


def partial_kernel(cap, got_hbm, pol_ref, stat_ref, rows_ref, part_ref, meta_ref, got_ref, column_ref, load):
    slots, columns = pol_ref.shape
    blocks = columns // LANES
    owners = got_ref.shape[0]
    tall = GROUP * cap
    wide = OCTET * cap
    groups = got_ref.shape[1] // tall
    base = lax.axis_index("tp") * columns
    loads = []
    for o in range(owners // OCTET):
        part = pl.ds(o * OCTET, OCTET)
        loads.append(pltpu.make_async_copy(got_hbm.at[part], got_ref.at[part], load.at[o]))
        loads[-1].start()

    size = OCTET * tall
    a = iota((GROUP, wide, size), 0)
    b = iota((GROUP, wide, size), 1)
    target = b + cap * a
    for d in range(1, OCTET):
        target = target + jnp.where(b >= d * cap, tall - cap, 0)
    order = (target == iota((GROUP, wide, size), 2)).astype(f32).reshape(size, size).astype(bf16)
    lane = iota((wide, LANES), 1)

    for o in range(owners // OCTET):
        at = slice(o * wide, (o + 1) * wide)
        stat = stat_ref[at, :]
        peak = jnp.broadcast_to(stat[:, 0:1], (wide, LANES))
        loads[o].wait()

        def arrived(g):
            pair = [
                got_ref[o * OCTET : (o + 1) * OCTET, (g + h) * tall : (g + h + 1) * tall, :]
                .astype(f32)
                .reshape(size, LANES)
                .astype(bf16)
                for h in range(2)
            ]
            return jnp.dot(order, jnp.concatenate(pair, axis=1), preferred_element_type=f32)

        token = None
        top = jnp.full((wide, LANES), -jnp.inf, f32)
        cross = jnp.zeros((wide, LANES), f32)
        picked = jnp.zeros((wide, LANES), f32)
        info = counts = None
        for g in range(groups - 2, -1, -2):
            product = arrived(g)
            pieces = {
                (g + h) * GROUP + c: product[c * wide : (c + 1) * wide, h * LANES : (h + 1) * LANES]
                for h in range(2)
                for c in range(GROUP)
            }
            if blocks in pieces:
                info, counts = pieces[blocks], pieces[blocks + 1]
                column = (info[:, 0:1] + 256.0 * info[:, 1:2] + 65536.0 * info[:, 2:3]).astype(i32) - base
                token = jnp.broadcast_to(column, (wide, LANES)) - lane
            for c in sorted(n for n in pieces if n < blocks):
                q = pieces[c]
                span = slice(c * LANES, (c + 1) * LANES)
                z = pol_ref[at, span].astype(f32)
                rows_ref[at, span] = q.astype(bf16)
                top = jnp.maximum(top, q)
                cross = cross + jnp.exp(z - peak) * (z - q)
                picked = jnp.where(token == c * LANES, z, picked)
        top = jnp.max(top, axis=1, keepdims=True)
        total = jnp.zeros((wide, LANES), f32)
        for c in range(blocks):
            total = total + jnp.exp(rows_ref[at, c * LANES : (c + 1) * LANES].astype(f32) - top)
        sums = (
            jnp.sum(cross, axis=1, keepdims=True),
            jnp.sum(picked, axis=1, keepdims=True),
            top,
            jnp.sum(total, axis=1, keepdims=True),
            info[:, 3:4],
            info[:, 4:5],
            column.astype(f32),
            counts[:, 0:1],
        )
        out = stat
        for n, value in enumerate(sums):
            out = jnp.where(lane == 2 + n, value, out)
        column_ref[at, :] = out
    column_ref[slots:, :] = jnp.ones((column_ref.shape[0] - slots, LANES), f32)
    turned = column_ref[...].T
    peak, total, cross, picked, top, total_q = (turned[n : n + 1, :] for n in range(6))
    values = (peak + jnp.log(total), cross / total, picked, top + jnp.log(total_q))
    for n, value in enumerate(values):
        part_ref[:, n : n + 1, :] = jnp.broadcast_to(value[None], (part_ref.shape[0],) + value.shape)
    for n in range(4):
        meta_ref[n : n + 1, :] = turned[6 + n : 7 + n, :]
    meta_ref[4:5, :] = peak


def grad_kernel(
    cap, row_total, all_ref, meta_ref, rewards_ref, group_ref, pol_ref, rows_ref, grad_hbm, loss_ref, turn_ref, column_ref, grad_ref, store
):
    slots, columns = pol_ref.shape
    blocks = columns // LANES
    seqs = rewards_ref.shape[0]
    wide = OCTET * cap
    padded = meta_ref.shape[1]

    rewards = rewards_ref[...].reshape(1, seqs)
    groups = group_ref[...].reshape(1, seqs)
    diagonal = iota((seqs, seqs), 0) == iota((seqs, seqs), 1)
    group_down = jnp.sum(jnp.where(diagonal, groups, 0), axis=1, keepdims=True)
    reward_down = jnp.sum(jnp.where(diagonal, rewards, 0.0), axis=1, keepdims=True)
    same = (group_down == groups).astype(f32)
    mean = jnp.sum(same * rewards, axis=1, keepdims=True) / jnp.sum(same, axis=1, keepdims=True)
    advantage = reward_down - mean

    old, tag, token, counts, mine = (meta_ref[n : n + 1, :] for n in range(5))
    valid = tag > 0.5
    adv = jnp.sum(
        jnp.where(iota((seqs, padded), 0) + 1 == tag.astype(i32), advantage, 0.0), axis=0, keepdims=True
    )
    valid_total = jnp.sum(jnp.where(iota((1, padded), 1) < slots, counts, 0.0)) / cap

    logs, gaps, tokens, logs_q = (all_ref[:, n, :] for n in range(4))
    peak = jnp.max(logs, axis=0, keepdims=True)
    weight = jnp.exp(logs - peak)
    total = jnp.sum(weight, axis=0, keepdims=True)
    gap = jnp.sum(gaps * weight, axis=0, keepdims=True) / total
    log_p = peak + jnp.log(total)
    peak_q = jnp.max(logs_q, axis=0, keepdims=True)
    log_q = peak_q + jnp.log(jnp.sum(jnp.exp(logs_q - peak_q), axis=0, keepdims=True))
    kl_term = gap - log_p + log_q
    raw = jnp.sum(tokens, axis=0, keepdims=True) - log_p - old
    ratio = jnp.exp(jnp.clip(raw, -ratio_clamp, ratio_clamp))
    plain = -adv * ratio
    clipped = -adv * jnp.clip(ratio, low_bound, high_bound)
    upper = jnp.maximum(plain, clipped)
    dual = -dual_bound * adv
    negative = adv < 0.0
    loss = jnp.where(negative, jnp.minimum(upper, dual), upper)
    loss_ref[...] = jnp.where(valid, loss + kl_weight * kl_term, 0.0)[:, :slots].reshape(slots)
    inside = (ratio > low_bound) & (ratio < high_bound)
    coef = jnp.where((plain >= clipped) | inside, plain, 0.0)
    coef = jnp.where(negative & (upper > dual), 0.0, coef)
    coef = jnp.where(jnp.abs(raw) < ratio_clamp, coef, 0.0)
    scale = jnp.where(valid, row_total / valid_total, 0.0)
    turn_ref[...] = jnp.zeros(turn_ref.shape, f32)
    share = scale * jnp.exp(mine - peak) / total
    for n, value in enumerate((share * kl_weight, share * coef, scale * coef, gap, token, mine)):
        turn_ref[n : n + 1, :] = value
    column_ref[...] = turn_ref[...].T
    lane = iota((wide, LANES), 1)
    stores = []
    for o in range(slots // wide):
        at = slice(o * wide, (o + 1) * wide)
        slope, level, spike, gaps, col, top = (
            jnp.broadcast_to(column_ref[at, n : n + 1], (wide, LANES)) for n in range(6)
        )
        where = col.astype(i32) - lane
        for c in range(blocks):
            span = slice(c * LANES, (c + 1) * LANES)
            z = pol_ref[at, span].astype(f32)
            q = rows_ref[at, span].astype(f32)
            out = jnp.exp(z - top) * (slope * ((z - q) - gaps) - level)
            out = out + jnp.where(where == c * LANES, spike, 0.0)
            grad_ref[at, span] = out.astype(bf16)
        stores.append(pltpu.make_async_copy(grad_ref.at[at], grad_hbm.at[at], store.at[o]))
        stores[-1].start()
    for copy in stores:
        copy.wait()


def call(kernel, out_shape, ins, outs, scratch=(), cost=None, limit=VMEM_LIMIT):
    spec = {"h": pl.BlockSpec(memory_space=pltpu.HBM), "v": pl.BlockSpec(memory_space=pltpu.VMEM)}
    return pl.pallas_call(
        kernel,
        out_shape=out_shape,
        in_specs=[spec[n] for n in ins],
        out_specs=[spec[n] for n in outs],
        scratch_shapes=list(scratch),
        compiler_params=pltpu.CompilerParams(vmem_limit_bytes=limit),
        cost_estimate=cost,
    )


def shards(ref_logits, token_ids, old_logp, owner_of_row, lengths, rewards, group_ids, pol_logits):
    owners = lax.axis_size("role") * lax.axis_size("dp")
    return steps(owners, ref_logits, token_ids, old_logp, owner_of_row, lengths, rewards, group_ids, pol_logits)


def steps(owners, ref_logits, token_ids, old_logp, owner_of_row, lengths, rewards, group_ids, pol_logits):
    peers = lax.axis_size("tp")
    rows, columns = ref_logits.shape
    slots = pol_logits.shape[0]
    cap = slots // owners
    blocks = columns // LANES
    groups = -(-(blocks + 2) // (2 * GROUP)) * 2
    deep = groups * GROUP * cap
    padded = -(-slots // LANES) * LANES
    shape = jax.ShapeDtypeStruct
    vmem = pltpu.VMEM
    sems = lambda n: pltpu.SemaphoreType.DMA((n,))
    everyone = ("role", "dp")
    octets = owners // OCTET

    [send] = call(
        functools.partial(send_kernel, cap),
        [shape((owners, deep, LANES), bf16)],
        "hhhhh",
        "h",
        (
            vmem((rows,), i32),
            vmem((rows,), bf16),
            vmem((rows,), i32),
            pltpu.SMEM(lengths.shape, i32),
            vmem((rows, columns), bf16),
            vmem((owners, deep, LANES), bf16),
            sems(4),
            sems(groups // 2),
            sems(groups // 2),
        ),
        limit=WHOLE_VMEM,
    )(token_ids, old_logp, owner_of_row, lengths, ref_logits)
    got = lax.all_to_all(send, everyone, split_axis=0, concat_axis=0, tiled=True)
    [stats] = call(
        policy_kernel,
        [shape((slots, LANES), f32)],
        "v",
        "v",
        cost=pl.CostEstimate(
            flops=8 * slots * columns, bytes_accessed=2 * slots * columns, transcendentals=slots * columns
        ),
    )(pol_logits)
    got_rows, parts, meta = call(
        functools.partial(partial_kernel, cap),
        [shape((slots, columns), bf16), shape((peers, 4, padded), f32), shape((8, padded), f32)],
        "hvv",
        "vvv",
        (vmem((owners, deep, LANES), bf16), vmem((padded, LANES), f32), sems(octets)),
    )(got, pol_logits, stats)
    everything = lax.all_to_all(parts, "tp", split_axis=0, concat_axis=0, tiled=True)
    return call(
        functools.partial(grad_kernel, cap, float(rows * owners)),
        [shape((slots, columns), bf16), shape((slots,), f32)],
        "vvvvvv",
        "hv",
        (vmem((LANES, padded), f32), vmem((padded, LANES), f32), vmem((slots, columns), bf16), sems(octets)),
    )(everything, meta, rewards, group_ids, pol_logits, got_rows)


def solution(mesh):
    return jax.shard_map(
        shards,
        mesh=mesh,
        in_specs=(
            P(("role", "dp"), "tp"),
            P(("role", "dp")),
            P(("role", "dp")),
            P(("role", "dp")),
            P(("role", "dp")),
            P(),
            P(),
            P(("role", "dp"), "tp"),
        ),
        out_specs=(P(("role", "dp"), "tp"), P(("role", "dp"))),
        check_vma=False,
    )
```

time: 82.2 us -> 75.6 us (0.920)
  local copies, waits for them, and re-layouts: 9.05 us -> 0.01 us
  waiting for transfers between devices: 25.1 us -> 26.9 us
  Pallas kernels: 11.9 us -> 13.3 us
    unnamed x22 -> x6, local copies, waits for them, and re-layouts: 9.05 us -> 0.01 us
    all_to_all x1, waiting for transfers between devices: 25.1 us -> 26.9 us  [steps(): lax.all_to_all(send, everyone, split_axis=0, concat_axis=0, tiled=True)]
    pallas_call x4, Pallas kernels: 11.9 us -> 13.3 us  [the longest x1 4.26 us: steps(): call(functools.partial(partial_kernel, cap), [shape((slots, columns), bf1...]
where the time goes in v2:
time: 75.6 us; the launch traced here: 75.3 us
  waiting for transfers between devices  26.9 us (36%)
  blocking collectives  26.8 us (35%)
  Pallas kernels  13.3 us (18%)
  starting transfers between devices  7.57 us (10%)
    all_to_all x1, waiting for transfers between devices, steps(): lax.all_to_all(send, everyone, split_axis=0, concat_axis=0, tiled=True)  26.9 us
    all_to_all x1, blocking collectives, steps(): lax.all_to_all(parts, 'tp', split_axis=0, concat_axis=0, tiled=True)  26.8 us
    all_to_all x1, starting transfers between devices, steps(): lax.all_to_all(send, everyone, split_axis=0, concat_axis=0, tiled=True)  7.57 us
    pallas_call x1, Pallas kernels, steps(): call(functools.partial(partial_kernel, cap), [shape((slots, columns), bf1...  4.26 us
    pallas_call x1, Pallas kernels, steps(): call(functools.partial(send_kernel, cap), [shape((owners, deep, LANES), b...  3.9 us
    pallas_call x1, Pallas kernels, steps(): call(functools.partial(grad_kernel, cap, float(rows * owners)), [shape((s...  3.67 us
  transfers between devices with their start and end apart: 1, of which 1 were waited for; matrix products, arithmetic and copies ran while one was open for 0% of the time, Pallas kernels for 2%

profile of v2, /device:TPU:32, one launch (start us, length us, event | category | flops | bytes accessed | tf_op | source)
XLA Modules:
  0.0 75.3 jit_solution(12339590763483742070)
XLA Ops:
  0.6 3.9 %shard_map.95 = bf16[32,240,128]{2,1,0:T(8,128)(2,1)} custom-call(s32[128]{0:T(128)} %ids_hbm.1, bf16[128]{0:T(256)(128)(2,1)} %old_hbm.1, s32[128]{0:T(128)} %owner_hbm.1, s32[2]{0:T(128)} %len_hbm.1, bf16[128,4864]{1,0:T(8,128)(2,1)} %ref_hbm.1), custom_call_target="tpu_custom_call" | custom-call | tf_op jit(solution)/shard_map/pallas_call | solution.py:352
  4.5 0.0 copy-start
  4.6 7.6 %all-to-all-start = ((bf16[32,240,128]{2,1,0:T(8,128)(2,1)}), bf16[32,240,128]{2,1,0:T(8,128)(2,1)}, u32[]{:S(2)}, u32[]{:S(2)}) async-start(bf16[32,240,128]{2,1,0:T(8,128)(2,1)} %shard_map.95), calls=%async_computation | async-start | bytes 3932160 | tf_op jit(solution)/shard_map/all_to_all | solution.py:370
  12.1 0.0 copy-done
  12.1 1.5 %shard_map.96.stat_ref = f32[192,128]{1,0:T(8,128)S(1)} custom-call(bf16[192,4864]{1,0:T(8,128)(2,1)S(1)} %copy-done), custom_call_target="tpu_custom_call" | custom-call | flops 7471104 | bytes 1867776 | tf_op jit(solution)/shard_map/pallas_call | solution.py:371
  13.6 0.0 copy-start.1
  13.6 0.0 copy-start.2
  13.6 26.9 %all-to-all-done.got_hbm = bf16[32,240,128]{2,1,0:T(8,128)(2,1)} async-done(((bf16[32,240,128]{2,1,0:T(8,128)(2,1)}), bf16[32,240,128]{2,1,0:T(8,128)(2,1)}, u32[]{:S(2)}, u32[]{:S(2)}) %all-to-all-start) | async-done | bytes 1966112 | tf_op jit(solution)/shard_map/all_to_all | solution.py:370
  40.5 4.3 %shard_map.97 = (bf16[192,4864]{1,0:T(8,128)(2,1)S(1)}, f32[16,4,256]{2,1,0:T(4,128)S(1)}, f32[8,256]{1,0:T(8,128)S(1)}) custom-call(bf16[32,240,128]{2,1,0:T(8,128)(2,1)} %all-to-all-done.got_hbm, bf16[192,4864]{1,0:T(8,128)(2,1)S(1)} %copy-done, f32[192,128]{1,0:T(8,128)S(1)} %shard_map.96.stat_ref), custom_call_target="tpu_custom_call" | custom-call | tf_op jit(solution)/shard_map/pallas_call | solution.py:380
  44.8 26.8 %all_to_all.10.all_ref = f32[16,4,256]{2,1,0:T(4,128)S(1)} all-to-all(f32[16,4,256]{2,1,0:T(4,128)S(1)} %get-tuple-element.5), channel_id=1, replica_groups=mesh['role'=4,'dp'=8,'tp'=16] {'tp'}, dimensions={0} | all-to-all | bytes 131072 | tf_op jit(solution)/shard_map/all_to_all | solution.py:387
  71.7 0.0 copy-done.1
  71.7 0.0 copy-done.2
  71.7 3.7 %shard_map.98 = (bf16[192,4864]{1,0:T(8,128)(2,1)}, f32[192]{0:T(256)}) custom-call(f32[16,4,256]{2,1,0:T(4,128)S(1)} %all_to_all.10.all_ref, f32[8,256]{1,0:T(8,128)S(1)} %get-tuple-element.6.meta_ref, f32[64]{0:T(128)S(1)} %copy-done.1, s32[64]{0:T(128)S(1)} %copy-done.2, bf16[192,4864]{1,0:T(8,128)(2,1)S(1)} %copy-done, ...), custom_call_target="tpu_custom_call" | custom-call | tf_op jit(solution)/shard_map/pallas_call | solution.py:388
Async XLA Ops:
  4.5 7.6 %copy-start = (bf16[192,4864]{1,0:T(8,128)(2,1)S(1)}, bf16[192,4864]{1,0:T(8,128)(2,1)}, u32[]{:S(2)}) copy-start(bf16[192,4864]{1,0:T(8,128)(2,1)} %pol_ref.5) | copy-start | bytes 5603332
  4.6 36.0 %all-to-all-start = ((bf16[32,240,128]{2,1,0:T(8,128)(2,1)}), bf16[32,240,128]{2,1,0:T(8,128)(2,1)}, u32[]{:S(2)}, u32[]{:S(2)}) async-start(bf16[32,240,128]{2,1,0:T(8,128)(2,1)} %shard_map.95), calls=%async_computation | async-start | bytes 3932160 | tf_op jit(solution)/shard_map/all_to_all | solution.py:370
  13.6 58.0 %copy-start.1 = (f32[64]{0:T(128)S(1)}, f32[64]{0:T(128)}, u32[]{:S(2)}) copy-start(f32[64]{0:T(128)} %rewards_ref.1) | copy-start | bytes 772
  13.6 58.0 %copy-start.2 = (s32[64]{0:T(128)S(1)}, s32[64]{0:T(128)}, u32[]{:S(2)}) copy-start(s32[64]{0:T(128)} %group_ref.1) | copy-start | bytes 772

commit v3 on v2

--- a/solution.py
+++ b/solution.py
@@ -16,6 +16,7 @@
 LANES = 128
 GROUP = 4
 OCTET = 8
+STORE_ROWS = 16
 VMEM_LIMIT = 16 * 1024 * 1024
 WHOLE_VMEM = 60 * 1024 * 1024
 
@@ -83,7 +84,8 @@
     )
     for n, value in enumerate(values):
         table = jnp.where(feature == n, value, table)
-    table = table.T.astype(bf16)
+    table = table.T
+    column = iota((rows, LANES), 1)
     nothing = jnp.zeros((rows, LANES), bf16)
 
     def block(c):
@@ -91,31 +93,46 @@
             return ref_ref[:, c * LANES : (c + 1) * LANES]
         return table if c == blocks else nothing
 
-    row = iota((OCTET, tall, rows), 1)
-    place = iota((OCTET, tall, rows), 0) * cap + row
+    half = tall - 8
+    row = iota((OCTET, half, rows), 1)
+    place = iota((OCTET, half, rows), 0) * cap + row
     pickers = []
     for o in range(owners // OCTET):
-        parts = []
-        for c in range(GROUP):
-            mine = (row >= c * cap) & (row < (c + 1) * cap)
-            hit = mine & (place + o * OCTET * cap == slot.reshape(1, 1, rows) + c * cap)
-            parts.append(hit.astype(f32).reshape(OCTET * tall, rows).astype(bf16))
-        pickers.append(jnp.concatenate(parts, axis=1))
+        for side in range(2):
+            parts = []
+            for c in range(2 * side, 2 * side + 2):
+                first = c * cap - 8 * side
+                mine = (row >= first) & (row < first + cap)
+                hit = mine & (place + (o * OCTET * cap - first) == slot.reshape(1, 1, rows))
+                parts.append(hit.astype(f32).reshape(OCTET * half, rows).astype(bf16))
+            pickers.append(jnp.concatenate(parts, axis=1))
     last_row = iota((OCTET, tall, LANES), 1)
+    highest = None
     stores = []
     for n, g in enumerate(range(0, groups, 2)):
         loads[n].wait()
-        right = jnp.concatenate(
-            [
-                jnp.concatenate([block((g + h) * GROUP + c) for h in range(2)], axis=1)
-                for c in range(GROUP)
-            ],
-            axis=0,
-        )
+        for c in range(g * GROUP, min((g + 2) * GROUP, blocks)):
+            highest = block(c) if highest is None else jnp.maximum(highest, block(c))
+        if (g + 2) * GROUP > blocks:
+            table = jnp.where(column == len(values), jnp.max(highest.astype(f32), axis=1, keepdims=True), table).astype(bf16)
+        right = [
+            jnp.concatenate(
+                [
+                    jnp.concatenate([block((g + h) * GROUP + 2 * side + c) for h in range(2)], axis=1)
+                    for c in range(2)
+                ],
+                axis=0,
+            )
+            for side in range(2)
+        ]
         for o in range(owners // OCTET):
-            out = jnp.dot(pickers[o], right, preferred_element_type=f32)
+            out = [
+                jnp.dot(pickers[2 * o + side], right[side], preferred_element_type=f32).reshape(OCTET, half, 2 * LANES)
+                for side in range(2)
+            ]
+            both = jnp.concatenate([out[0][:, 0:8], out[0][:, 8:] + out[1][:, : half - 8], out[1][:, half - 8 :]], axis=1)
             for h in range(2):
-                part = out[:, h * LANES : (h + 1) * LANES].reshape(OCTET, tall, LANES)
+                part = both[:, :, h * LANES : (h + 1) * LANES]
                 if (g + h + 1) * GROUP > blocks + 1:
                     first = (blocks + 1 - (g + h) * GROUP) * cap
                     part = jnp.where(last_row >= first, count.astype(f32), part)
@@ -129,28 +146,7 @@
         copy.wait()
 
 
-def policy_kernel(pol_ref, stat_ref):
-    slots, columns = pol_ref.shape
-    step = 48
-    lane = iota((step, LANES), 1)
-
-    def body(i, carry):
-        at = pl.ds(pl.multiple_of(i * step, 16), step)
-        top = pol_ref[at, 0:LANES].astype(f32)
-        for c in range(1, columns // LANES):
-            top = jnp.maximum(top, pol_ref[at, c * LANES : (c + 1) * LANES].astype(f32))
-        top = jnp.max(top, axis=1, keepdims=True)
-        total = jnp.zeros((step, LANES), f32)
-        for c in range(columns // LANES):
-            total = total + jnp.exp(pol_ref[at, c * LANES : (c + 1) * LANES].astype(f32) - top)
-        total = jnp.sum(total, axis=1, keepdims=True)
-        stat_ref[at, :] = jnp.where(lane == 0, top, jnp.where(lane == 1, total, 0.0))
-        return carry
-
-    lax.fori_loop(0, slots // step, body, 0)
-
-
-def partial_kernel(cap, got_hbm, pol_ref, stat_ref, rows_ref, part_ref, meta_ref, got_ref, column_ref, load):
+def partial_kernel(cap, got_ref, pol_ref, exp_ref, gap_ref, part_ref, meta_ref, column_ref):
     slots, columns = pol_ref.shape
     blocks = columns // LANES
     owners = got_ref.shape[0]
@@ -158,11 +154,6 @@
     wide = OCTET * cap
     groups = got_ref.shape[1] // tall
     base = lax.axis_index("tp") * columns
-    loads = []
-    for o in range(owners // OCTET):
-        part = pl.ds(o * OCTET, OCTET)
-        loads.append(pltpu.make_async_copy(got_hbm.at[part], got_ref.at[part], load.at[o]))
-        loads[-1].start()
 
     size = OCTET * tall
     a = iota((GROUP, wide, size), 0)
@@ -175,9 +166,11 @@
 
     for o in range(owners // OCTET):
         at = slice(o * wide, (o + 1) * wide)
-        stat = stat_ref[at, :]
-        peak = jnp.broadcast_to(stat[:, 0:1], (wide, LANES))
-        loads[o].wait()
+        highest = pol_ref[at, 0:LANES]
+        for c in range(1, blocks):
+            highest = jnp.maximum(highest, pol_ref[at, c * LANES : (c + 1) * LANES])
+        peak = jnp.max(highest.astype(f32), axis=1, keepdims=True)
+        peaks = jnp.broadcast_to(peak, (wide, LANES))
 
         def arrived(g):
             pair = [
@@ -190,9 +183,7 @@
             return jnp.dot(order, jnp.concatenate(pair, axis=1), preferred_element_type=f32)
 
         token = None
-        top = jnp.full((wide, LANES), -jnp.inf, f32)
-        cross = jnp.zeros((wide, LANES), f32)
-        picked = jnp.zeros((wide, LANES), f32)
+        total, cross, picked, total_q = (jnp.zeros((wide, LANES), f32) for _ in range(4))
         info = counts = None
         for g in range(groups - 2, -1, -2):
             product = arrived(g)
@@ -205,31 +196,35 @@
                 info, counts = pieces[blocks], pieces[blocks + 1]
                 column = (info[:, 0:1] + 256.0 * info[:, 1:2] + 65536.0 * info[:, 2:3]).astype(i32) - base
                 token = jnp.broadcast_to(column, (wide, LANES)) - lane
+                top = info[:, 5:6]
+                tops = jnp.broadcast_to(top, (wide, LANES))
             for c in sorted(n for n in pieces if n < blocks):
                 q = pieces[c]
                 span = slice(c * LANES, (c + 1) * LANES)
                 z = pol_ref[at, span].astype(f32)
-                rows_ref[at, span] = q.astype(bf16)
-                top = jnp.maximum(top, q)
-                cross = cross + jnp.exp(z - peak) * (z - q)
+                exps = jnp.exp(z - peaks)
+                gaps = exps * (z - q)
+                exp_ref[at, span] = exps
+                gap_ref[at, span] = gaps
+                total = total + exps
+                cross = cross + gaps
+                total_q = total_q + jnp.exp(q - tops)
                 picked = jnp.where(token == c * LANES, z, picked)
-        top = jnp.max(top, axis=1, keepdims=True)
-        total = jnp.zeros((wide, LANES), f32)
-        for c in range(blocks):
-            total = total + jnp.exp(rows_ref[at, c * LANES : (c + 1) * LANES].astype(f32) - top)
         sums = (
+            peak,
+            jnp.sum(total, axis=1, keepdims=True),
             jnp.sum(cross, axis=1, keepdims=True),
             jnp.sum(picked, axis=1, keepdims=True),
             top,
-            jnp.sum(total, axis=1, keepdims=True),
+            jnp.sum(total_q, axis=1, keepdims=True),
             info[:, 3:4],
             info[:, 4:5],
             column.astype(f32),
             counts[:, 0:1],
         )
-        out = stat
+        out = jnp.zeros((wide, LANES), f32)
         for n, value in enumerate(sums):
-            out = jnp.where(lane == 2 + n, value, out)
+            out = jnp.where(lane == n, value, out)
         column_ref[at, :] = out
     column_ref[slots:, :] = jnp.ones((column_ref.shape[0] - slots, LANES), f32)
     turned = column_ref[...].T
@@ -243,12 +238,11 @@
 
 
 def grad_kernel(
-    cap, row_total, all_ref, meta_ref, rewards_ref, group_ref, pol_ref, rows_ref, grad_hbm, loss_ref, turn_ref, column_ref, grad_ref, store
+    cap, row_total, all_ref, meta_ref, rewards_ref, group_ref, exp_ref, gap_ref, grad_hbm, loss_ref, turn_ref, column_ref, grad_ref, store
 ):
-    slots, columns = pol_ref.shape
+    slots, columns = exp_ref.shape
     blocks = columns // LANES
     seqs = rewards_ref.shape[0]
-    wide = OCTET * cap
     padded = meta_ref.shape[1]
 
     rewards = rewards_ref[...].reshape(1, seqs)
@@ -292,25 +286,25 @@
     scale = jnp.where(valid, row_total / valid_total, 0.0)
     turn_ref[...] = jnp.zeros(turn_ref.shape, f32)
     share = scale * jnp.exp(mine - peak) / total
-    for n, value in enumerate((share * kl_weight, share * coef, scale * coef, gap, token, mine)):
+    slope = share * kl_weight
+    for n, value in enumerate((slope, slope * gap + share * coef, scale * coef, token)):
         turn_ref[n : n + 1, :] = value
     column_ref[...] = turn_ref[...].T
-    lane = iota((wide, LANES), 1)
+    step = slots // store.shape[0]
+    lane = iota((step, LANES), 1)
     stores = []
-    for o in range(slots // wide):
-        at = slice(o * wide, (o + 1) * wide)
-        slope, level, spike, gaps, col, top = (
-            jnp.broadcast_to(column_ref[at, n : n + 1], (wide, LANES)) for n in range(6)
+    for i in range(slots // step):
+        at = slice(i * step, (i + 1) * step)
+        slope, level, spike, col = (
+            jnp.broadcast_to(column_ref[at, n : n + 1], (step, LANES)) for n in range(4)
         )
         where = col.astype(i32) - lane
         for c in range(blocks):
             span = slice(c * LANES, (c + 1) * LANES)
-            z = pol_ref[at, span].astype(f32)
-            q = rows_ref[at, span].astype(f32)
-            out = jnp.exp(z - top) * (slope * ((z - q) - gaps) - level)
+            out = slope * gap_ref[at, span] - level * exp_ref[at, span]
             out = out + jnp.where(where == c * LANES, spike, 0.0)
             grad_ref[at, span] = out.astype(bf16)
-        stores.append(pltpu.make_async_copy(grad_ref.at[at], grad_hbm.at[at], store.at[o]))
+        stores.append(pltpu.make_async_copy(grad_ref.at[at], grad_hbm.at[at], store.at[i]))
         stores[-1].start()
     for copy in stores:
         copy.wait()
@@ -347,7 +341,6 @@
     vmem = pltpu.VMEM
     sems = lambda n: pltpu.SemaphoreType.DMA((n,))
     everyone = ("role", "dp")
-    octets = owners // OCTET
 
     [send] = call(
         functools.partial(send_kernel, cap),
@@ -368,30 +361,27 @@
         limit=WHOLE_VMEM,
     )(token_ids, old_logp, owner_of_row, lengths, ref_logits)
     got = lax.all_to_all(send, everyone, split_axis=0, concat_axis=0, tiled=True)
-    [stats] = call(
-        policy_kernel,
-        [shape((slots, LANES), f32)],
-        "v",
-        "v",
-        cost=pl.CostEstimate(
-            flops=8 * slots * columns, bytes_accessed=2 * slots * columns, transcendentals=slots * columns
-        ),
-    )(pol_logits)
-    got_rows, parts, meta = call(
+    exps, gaps, parts, meta = call(
         functools.partial(partial_kernel, cap),
-        [shape((slots, columns), bf16), shape((peers, 4, padded), f32), shape((8, padded), f32)],
-        "hvv",
-        "vvv",
-        (vmem((owners, deep, LANES), bf16), vmem((padded, LANES), f32), sems(octets)),
-    )(got, pol_logits, stats)
+        [
+            shape((slots, columns), f32),
+            shape((slots, columns), f32),
+            shape((peers, 4, padded), f32),
+            shape((8, padded), f32),
+        ],
+        "vv",
+        "vvvv",
+        (vmem((padded, LANES), f32),),
+    )(got, pol_logits)
     everything = lax.all_to_all(parts, "tp", split_axis=0, concat_axis=0, tiled=True)
+    pieces = slots // STORE_ROWS
     return call(
         functools.partial(grad_kernel, cap, float(rows * owners)),
         [shape((slots, columns), bf16), shape((slots,), f32)],
         "vvvvvv",
         "hv",
-        (vmem((LANES, padded), f32), vmem((padded, LANES), f32), vmem((slots, columns), bf16), sems(octets)),
-    )(everything, meta, rewards, group_ids, pol_logits, got_rows)
+        (vmem((LANES, padded), f32), vmem((padded, LANES), f32), vmem((slots, columns), bf16), sems(pieces)),
+    )(everything, meta, rewards, group_ids, exps, gaps)
 
 
 def solution(mesh):

time: 75.6 us -> 72.3 us (0.956)
  the two profiles are of different devices: /device:TPU:32 before, /device:TPU:1 now
where the time goes in v3:
time: 72.3 us; the launch traced here: 72 us
  blocking collectives  62.1 us (86%)
  Pallas kernels  9.28 us (13%)
    all_to_all x1, blocking collectives, steps(): lax.all_to_all(send, everyone, split_axis=0, concat_axis=0, tiled=True)  37.8 us
    all_to_all x1, blocking collectives, steps(): lax.all_to_all(parts, 'tp', split_axis=0, concat_axis=0, tiled=True)  24.3 us
    pallas_call x1, Pallas kernels, steps(): call(functools.partial(send_kernel, cap), [shape((owners, deep, LANES), b...  3.75 us
    pallas_call x1, Pallas kernels, steps(): call(functools.partial(grad_kernel, cap, float(rows * owners)), [shape((s...  2.94 us
    pallas_call x1, Pallas kernels, steps(): call(functools.partial(partial_kernel, cap), [shape((slots, columns), f32...  2.59 us

profile of v3, /device:TPU:1, one launch (start us, length us, event | category | flops | bytes accessed | tf_op | source)
XLA Modules:
  0.0 72.0 jit_solution(893960595742877748)
XLA Ops:
  0.6 3.8 %shard_map.95 = bf16[32,240,128]{2,1,0:T(8,128)(2,1)} custom-call(s32[128]{0:T(128)} %ids_hbm.1, bf16[128]{0:T(256)(128)(2,1)} %old_hbm.1, s32[128]{0:T(128)} %owner_hbm.1, s32[2]{0:T(128)} %len_hbm.1, bf16[128,4864]{1,0:T(8,128)(2,1)} %ref_hbm.1), custom_call_target="tpu_custom_call" | custom-call | tf_op jit(solution)/shard_map/pallas_call | solution.py:345
  4.4 0.0 copy-start
  4.4 37.8 %all_to_all.10.got_ref = bf16[32,240,128]{2,1,0:T(8,128)(2,1)S(1)} all-to-all(bf16[32,240,128]{2,1,0:T(8,128)(2,1)} %shard_map.95), channel_id=1, replica_groups=mesh['role'=4,'dp'=8,'tp'=16] {'role','dp'}, dimensions={0} | all-to-all | bytes 3932160 | tf_op jit(solution)/shard_map/all_to_all | solution.py:363
  42.2 0.0 copy-done
  42.2 0.0 copy-start.1
  42.2 0.0 copy-start.2
  42.2 2.6 %shard_map.96 = (f32[192,4864]{1,0:T(8,128)S(1)}, f32[192,4864]{1,0:T(8,128)S(1)}, f32[16,4,256]{2,1,0:T(4,128)S(1)}, f32[8,256]{1,0:T(8,128)S(1)}) custom-call(bf16[32,240,128]{2,1,0:T(8,128)(2,1)S(1)} %all_to_all.10.got_ref, bf16[192,4864]{1,0:T(8,128)(2,1)S(1)} %copy-done), custom_call_target="tpu_custom_call" | custom-call | tf_op jit(solution)/shard_map/pallas_call | solution.py:364
  44.8 24.3 %all_to_all.11.all_ref = f32[16,4,256]{2,1,0:T(4,128)S(1)} all-to-all(f32[16,4,256]{2,1,0:T(4,128)S(1)} %get-tuple-element.6), channel_id=1, replica_groups=mesh['role'=4,'dp'=8,'tp'=16] {'tp'}, dimensions={0} | all-to-all | bytes 131072 | tf_op jit(solution)/shard_map/all_to_all | solution.py:376
  69.1 0.0 copy-done.1
  69.1 0.0 copy-done.2
  69.1 2.9 %shard_map.97 = (bf16[192,4864]{1,0:T(8,128)(2,1)}, f32[192]{0:T(256)}) custom-call(f32[16,4,256]{2,1,0:T(4,128)S(1)} %all_to_all.11.all_ref, f32[8,256]{1,0:T(8,128)S(1)} %get-tuple-element.7.meta_ref, f32[64]{0:T(128)S(1)} %copy-done.1, s32[64]{0:T(128)S(1)} %copy-done.2, f32[192,4864]{1,0:T(8,128)S(1)} %get-tuple-element.8.exp_ref, ...), custom_call_target="tpu_custom_call" | custom-call | tf_op jit(solution)/shard_map/pallas_call | solution.py:378
Async XLA Ops:
  4.4 37.8 %copy-start = (bf16[192,4864]{1,0:T(8,128)(2,1)S(1)}, bf16[192,4864]{1,0:T(8,128)(2,1)}, u32[]{:S(2)}) copy-start(bf16[192,4864]{1,0:T(8,128)(2,1)} %pol_ref.1) | copy-start | bytes 5603332
  42.2 26.9 %copy-start.1 = (f32[64]{0:T(128)S(1)}, f32[64]{0:T(128)}, u32[]{:S(2)}) copy-start(f32[64]{0:T(128)} %rewards_ref.1) | copy-start | bytes 772
  42.2 26.9 %copy-start.2 = (s32[64]{0:T(128)S(1)}, s32[64]{0:T(128)}, u32[]{:S(2)}) copy-start(s32[64]{0:T(128)} %group_ref.1) | copy-start | bytes 772

commit v4 on v3

--- a/solution.py
+++ b/solution.py
@@ -15,10 +15,10 @@
 
 LANES = 128
 GROUP = 4
+HALF = 64
 OCTET = 8
 STORE_ROWS = 16
 VMEM_LIMIT = 16 * 1024 * 1024
-WHOLE_VMEM = 60 * 1024 * 1024
 
 f32 = jnp.float32
 bf16 = jnp.bfloat16
@@ -30,13 +30,13 @@
 
 
 def send_kernel(
-    cap, ids_hbm, old_hbm, owner_hbm, len_hbm, ref_hbm, send_hbm, ids_ref, old_ref, owner_ref, len_ref, ref_ref, send_ref, small, load, store
+    cap, ids_hbm, old_hbm, owner_hbm, len_hbm, ref_hbm, send_ref, ids_ref, old_ref, owner_ref, len_ref, ref_ref, small, load
 ):
     rows = ref_ref.shape[0]
     blocks = ref_ref.shape[1] // LANES
     owners = send_ref.shape[0]
     tall = GROUP * cap
-    groups = send_ref.shape[1] // tall
+    full = blocks // GROUP
     seq_local = len_ref.shape[0]
     span = rows // seq_local
     me = lax.axis_index("role") * lax.axis_size("dp") + lax.axis_index("dp")
@@ -48,7 +48,7 @@
         )
     ]
     loads = []
-    for n, g in enumerate(range(0, groups, 2)):
+    for n, g in enumerate(range(0, full, 2)):
         part = slice(g * GROUP * LANES, min((g + 2) * GROUP, blocks) * LANES)
         loads.append(pltpu.make_async_copy(ref_hbm.at[:, part], ref_ref.at[:, part], load.at[n]))
     for copy in smalls + loads:
@@ -81,17 +81,17 @@
         (ids >> 16).astype(f32),
         old_ref[...].reshape(1, rows).astype(f32),
         tag.astype(f32),
+        jnp.ones((1, rows), f32),
     )
+    place_of = feature - (slot & 1) * HALF
     for n, value in enumerate(values):
-        table = jnp.where(feature == n, value, table)
+        table = jnp.where(place_of == n, value, table)
     table = table.T
-    column = iota((rows, LANES), 1)
+    column = iota((rows, LANES), 1) & (HALF - 1)
     nothing = jnp.zeros((rows, LANES), bf16)
 
     def block(c):
-        if c < blocks:
-            return ref_ref[:, c * LANES : (c + 1) * LANES]
-        return table if c == blocks else nothing
+        return ref_ref[:, c * LANES : (c + 1) * LANES] if c < blocks else nothing
 
     half = tall - 8
     row = iota((OCTET, half, rows), 1)
@@ -106,15 +106,13 @@
                 hit = mine & (place + (o * OCTET * cap - first) == slot.reshape(1, 1, rows))
                 parts.append(hit.astype(f32).reshape(OCTET * half, rows).astype(bf16))
             pickers.append(jnp.concatenate(parts, axis=1))
-    last_row = iota((OCTET, tall, LANES), 1)
+    last_row = iota((OCTET, half, LANES), 1)
     highest = None
-    stores = []
-    for n, g in enumerate(range(0, groups, 2)):
+    tails = []
+    for n, g in enumerate(range(0, full, 2)):
         loads[n].wait()
         for c in range(g * GROUP, min((g + 2) * GROUP, blocks)):
             highest = block(c) if highest is None else jnp.maximum(highest, block(c))
-        if (g + 2) * GROUP > blocks:
-            table = jnp.where(column == len(values), jnp.max(highest.astype(f32), axis=1, keepdims=True), table).astype(bf16)
         right = [
             jnp.concatenate(
                 [
@@ -131,19 +129,21 @@
                 for side in range(2)
             ]
             both = jnp.concatenate([out[0][:, 0:8], out[0][:, 8:] + out[1][:, : half - 8], out[1][:, half - 8 :]], axis=1)
-            for h in range(2):
-                part = both[:, :, h * LANES : (h + 1) * LANES]
-                if (g + h + 1) * GROUP > blocks + 1:
-                    first = (blocks + 1 - (g + h) * GROUP) * cap
-                    part = jnp.where(last_row >= first, count.astype(f32), part)
-                send_ref[
-                    o * OCTET : (o + 1) * OCTET, (g + h) * tall : (g + h + 1) * tall, :
-                ] = part.astype(bf16)
-        part = pl.ds(g * tall, 2 * tall)
-        stores.append(pltpu.make_async_copy(send_ref.at[:, part, :], send_hbm.at[:, part, :], store.at[n]))
-        stores[-1].start()
-    for copy in stores:
-        copy.wait()
+            for h in range(min(2, full - g)):
+                send_ref[o * OCTET : (o + 1) * OCTET, (g + h) * tall : (g + h + 1) * tall, :] = both[
+                    :, :, h * LANES : (h + 1) * LANES
+                ].astype(bf16)
+            if g + 2 > full:
+                tails.append(out[0][:, :, LANES:])
+    top = jnp.max(highest.astype(f32), axis=1, keepdims=True)
+    table = jnp.where(column == len(values) - 1, table * top, table).astype(bf16)
+    for o in range(owners // OCTET):
+        pair = iota((OCTET, half, rows), 0) * (cap // 2) + row + (o * OCTET * (cap // 2) - 2 * cap)
+        hit = (row >= 2 * cap) & (row < half - 1) & (pair == (slot >> 1).reshape(1, 1, rows))
+        picker = hit.astype(f32).reshape(OCTET * half, rows).astype(bf16)
+        extra = jnp.dot(picker, table, preferred_element_type=f32).reshape(OCTET, half, LANES)
+        tail = jnp.where(last_row == half - 1, count.astype(f32), tails[o] + extra)
+        send_ref[o * OCTET : (o + 1) * OCTET, full * tall :, :] = tail.astype(bf16)
 
 
 def partial_kernel(cap, got_ref, pol_ref, exp_ref, gap_ref, part_ref, meta_ref, column_ref):
@@ -152,7 +152,8 @@
     owners = got_ref.shape[0]
     tall = GROUP * cap
     wide = OCTET * cap
-    groups = got_ref.shape[1] // tall
+    full = blocks // GROUP
+    half = tall - 8
     base = lax.axis_index("tp") * columns
 
     size = OCTET * tall
@@ -162,7 +163,19 @@
     for d in range(1, OCTET):
         target = target + jnp.where(b >= d * cap, tall - cap, 0)
     order = (target == iota((GROUP, wide, size), 2)).astype(f32).reshape(size, size).astype(bf16)
+    small = OCTET * half
+    a = iota((3, wide, small), 0)
+    b = iota((3, wide, small), 1)
+    slot_row = b
+    source = jnp.zeros_like(b)
+    for d in range(1, OCTET):
+        slot_row = slot_row - jnp.where(b >= d * cap, cap, 0)
+        source = source + jnp.where(b >= d * cap, half, 0)
+    source = source + jnp.where(a == 2, 2 * cap + (slot_row >> 1), a * cap + slot_row)
+    tail_order = (source == iota((3, wide, small), 2)).astype(f32).reshape(3 * wide, small).astype(bf16)
     lane = iota((wide, LANES), 1)
+    odd = (iota((wide, LANES), 0) & 1) == 1
+    counts = jnp.zeros((1, LANES), f32)
 
     for o in range(owners // OCTET):
         at = slice(o * wide, (o + 1) * wide)
@@ -172,33 +185,40 @@
         peak = jnp.max(highest.astype(f32), axis=1, keepdims=True)
         peaks = jnp.broadcast_to(peak, (wide, LANES))
 
-        def arrived(g):
-            pair = [
-                got_ref[o * OCTET : (o + 1) * OCTET, (g + h) * tall : (g + h + 1) * tall, :]
+        def arrived(first, rows, ways, matrix):
+            parts = [
+                got_ref[o * OCTET : (o + 1) * OCTET, first + h * rows : first + (h + 1) * rows, :]
                 .astype(f32)
-                .reshape(size, LANES)
+                .reshape(OCTET * rows, LANES)
                 .astype(bf16)
-                for h in range(2)
+                for h in range(ways)
             ]
-            return jnp.dot(order, jnp.concatenate(pair, axis=1), preferred_element_type=f32)
-
-        token = None
+            right = jnp.concatenate(parts, axis=1) if ways > 1 else parts[0]
+            return jnp.dot(matrix, right, preferred_element_type=f32)
+
+        product = arrived(full * tall, half, 1, tail_order)
+        todo = [{full * GROUP + c: product[c * wide : (c + 1) * wide] for c in range(2)}]
+        info = product[2 * wide :]
+        info = jnp.where(odd, pltpu.roll(info, HALF, 1), info)
+        last = got_ref[o * OCTET : (o + 1) * OCTET, full * tall + 8 :, :].astype(f32)
+        counts = counts + jnp.sum(last[:, half - 9, :], axis=0, keepdims=True)
+        column = (info[:, 0:1] + 256.0 * info[:, 1:2] + 65536.0 * info[:, 2:3]).astype(i32) - base
+        token = jnp.broadcast_to(column, (wide, LANES)) - lane
+        top = info[:, 5:6]
+        tops = jnp.broadcast_to(top, (wide, LANES))
         total, cross, picked, total_q = (jnp.zeros((wide, LANES), f32) for _ in range(4))
-        info = counts = None
-        for g in range(groups - 2, -1, -2):
-            product = arrived(g)
-            pieces = {
-                (g + h) * GROUP + c: product[c * wide : (c + 1) * wide, h * LANES : (h + 1) * LANES]
-                for h in range(2)
-                for c in range(GROUP)
-            }
-            if blocks in pieces:
-                info, counts = pieces[blocks], pieces[blocks + 1]
-                column = (info[:, 0:1] + 256.0 * info[:, 1:2] + 65536.0 * info[:, 2:3]).astype(i32) - base
-                token = jnp.broadcast_to(column, (wide, LANES)) - lane
-                top = info[:, 5:6]
-                tops = jnp.broadcast_to(top, (wide, LANES))
-            for c in sorted(n for n in pieces if n < blocks):
+        for g in range(full - 1, -1, -2):
+            ways = 2 if g else 1
+            product = arrived((g - ways + 1) * tall, tall, ways, order)
+            todo.append(
+                {
+                    (g - ways + 1 + h) * GROUP + c: product[c * wide : (c + 1) * wide, h * LANES : (h + 1) * LANES]
+                    for h in range(ways)
+                    for c in range(GROUP)
+                }
+            )
+        for pieces in todo:
+            for c in sorted(pieces):
                 q = pieces[c]
                 span = slice(c * LANES, (c + 1) * LANES)
                 z = pol_ref[at, span].astype(f32)
@@ -220,7 +240,6 @@
             info[:, 3:4],
             info[:, 4:5],
             column.astype(f32),
-            counts[:, 0:1],
         )
         out = jnp.zeros((wide, LANES), f32)
         for n, value in enumerate(sums):
@@ -229,21 +248,22 @@
     column_ref[slots:, :] = jnp.ones((column_ref.shape[0] - slots, LANES), f32)
     turned = column_ref[...].T
     peak, total, cross, picked, top, total_q = (turned[n : n + 1, :] for n in range(6))
-    values = (peak + jnp.log(total), cross / total, picked, top + jnp.log(total_q))
-    for n, value in enumerate(values):
-        part_ref[:, n : n + 1, :] = jnp.broadcast_to(value[None], (part_ref.shape[0],) + value.shape)
-    for n in range(4):
+    pairs = ((peak + jnp.log(total), cross / total), (picked, top + jnp.log(total_q)))
+    for n, pair in enumerate(pairs):
+        line = jnp.concatenate([value[:, :slots] for value in pair], axis=1)
+        part_ref[:, n : n + 1, :] = jnp.broadcast_to(line[None], (part_ref.shape[0],) + line.shape)
+    for n in range(3):
         meta_ref[n : n + 1, :] = turned[6 + n : 7 + n, :]
+    meta_ref[3:4, :] = jnp.concatenate([counts] * (meta_ref.shape[1] // LANES), axis=1)
     meta_ref[4:5, :] = peak
 
 
 def grad_kernel(
-    cap, row_total, all_ref, meta_ref, rewards_ref, group_ref, exp_ref, gap_ref, grad_hbm, loss_ref, turn_ref, column_ref, grad_ref, store
+    row_total, all_ref, meta_ref, rewards_ref, group_ref, exp_ref, gap_ref, grad_hbm, loss_ref, turn_ref, column_ref, grad_ref, store
 ):
     slots, columns = exp_ref.shape
     blocks = columns // LANES
     seqs = rewards_ref.shape[0]
-    padded = meta_ref.shape[1]
 
     rewards = rewards_ref[...].reshape(1, seqs)
     groups = group_ref[...].reshape(1, seqs)
@@ -254,14 +274,13 @@
     mean = jnp.sum(same * rewards, axis=1, keepdims=True) / jnp.sum(same, axis=1, keepdims=True)
     advantage = reward_down - mean
 
-    old, tag, token, counts, mine = (meta_ref[n : n + 1, :] for n in range(5))
+    old, tag, token, valid_total, mine = (meta_ref[n : n + 1, :slots] for n in range(5))
     valid = tag > 0.5
     adv = jnp.sum(
-        jnp.where(iota((seqs, padded), 0) + 1 == tag.astype(i32), advantage, 0.0), axis=0, keepdims=True
+        jnp.where(iota((seqs, slots), 0) + 1 == tag.astype(i32), advantage, 0.0), axis=0, keepdims=True
     )
-    valid_total = jnp.sum(jnp.where(iota((1, padded), 1) < slots, counts, 0.0)) / cap
-
-    logs, gaps, tokens, logs_q = (all_ref[:, n, :] for n in range(4))
+
+    logs, gaps, tokens, logs_q = (all_ref[:, n, m * slots : (m + 1) * slots] for n in range(2) for m in range(2))
     peak = jnp.max(logs, axis=0, keepdims=True)
     weight = jnp.exp(logs - peak)
     total = jnp.sum(weight, axis=0, keepdims=True)
@@ -278,7 +297,7 @@
     dual = -dual_bound * adv
     negative = adv < 0.0
     loss = jnp.where(negative, jnp.minimum(upper, dual), upper)
-    loss_ref[...] = jnp.where(valid, loss + kl_weight * kl_term, 0.0)[:, :slots].reshape(slots)
+    loss_ref[...] = jnp.where(valid, loss + kl_weight * kl_term, 0.0).reshape(slots)
     inside = (ratio > low_bound) & (ratio < high_bound)
     coef = jnp.where((plain >= clipped) | inside, plain, 0.0)
     coef = jnp.where(negative & (upper > dual), 0.0, coef)
@@ -288,7 +307,7 @@
     share = scale * jnp.exp(mine - peak) / total
     slope = share * kl_weight
     for n, value in enumerate((slope, slope * gap + share * coef, scale * coef, token)):
-        turn_ref[n : n + 1, :] = value
+        turn_ref[n : n + 1, :slots] = value
     column_ref[...] = turn_ref[...].T
     step = slots // store.shape[0]
     lane = iota((step, LANES), 1)
@@ -334,8 +353,8 @@
     slots = pol_logits.shape[0]
     cap = slots // owners
     blocks = columns // LANES
-    groups = -(-(blocks + 2) // (2 * GROUP)) * 2
-    deep = groups * GROUP * cap
+    full = blocks // GROUP
+    deep = blocks * cap + 4
     padded = -(-slots // LANES) * LANES
     shape = jax.ShapeDtypeStruct
     vmem = pltpu.VMEM
@@ -346,27 +365,25 @@
         functools.partial(send_kernel, cap),
         [shape((owners, deep, LANES), bf16)],
         "hhhhh",
-        "h",
+        "v",
         (
             vmem((rows,), i32),
             vmem((rows,), bf16),
             vmem((rows,), i32),
             pltpu.SMEM(lengths.shape, i32),
             vmem((rows, columns), bf16),
-            vmem((owners, deep, LANES), bf16),
             sems(4),
-            sems(groups // 2),
-            sems(groups // 2),
+            sems(full // 2 + 1),
         ),
-        limit=WHOLE_VMEM,
-    )(token_ids, old_logp, owner_of_row, lengths, ref_logits)
+        limit=VMEM_LIMIT,
+    )(*(pltpu.with_memory_space_constraint(x, pltpu.HBM) for x in (token_ids, old_logp, owner_of_row, lengths, ref_logits)))
     got = lax.all_to_all(send, everyone, split_axis=0, concat_axis=0, tiled=True)
     exps, gaps, parts, meta = call(
         functools.partial(partial_kernel, cap),
         [
             shape((slots, columns), f32),
             shape((slots, columns), f32),
-            shape((peers, 4, padded), f32),
+            shape((peers, 2, 2 * slots), f32),
             shape((8, padded), f32),
         ],
         "vv",
@@ -376,7 +393,7 @@
     everything = lax.all_to_all(parts, "tp", split_axis=0, concat_axis=0, tiled=True)
     pieces = slots // STORE_ROWS
     return call(
-        functools.partial(grad_kernel, cap, float(rows * owners)),
+        functools.partial(grad_kernel, float(rows * owners)),
         [shape((slots, columns), bf16), shape((slots,), f32)],
         "vvvvvv",
         "hv",

time: 72.3 us -> 70.3 us (0.972)
  blocking collectives: 62.1 us -> 60.9 us
    all_to_all x1, blocking collectives: 37.8 us -> 35.9 us  [steps(): lax.all_to_all(send, everyone, split_axis=0, concat_axis=0, tiled=True)]
    pallas_call x1, Pallas kernels: 3.75 us -> 2.78 us  [steps(): call(functools.partial(send_kernel, cap), [shape((owners, deep, LANES), b...]
    all_to_all x1, blocking collectives: 24.3 us -> 25 us  [steps(): lax.all_to_all(parts, 'tp', split_axis=0, concat_axis=0, tiled=True)]
where the time goes in v4:
time: 70.3 us; the launch traced here: 70.1 us
  blocking collectives  60.9 us (87%)
  Pallas kernels  8.57 us (12%)
    all_to_all x1, blocking collectives, steps(): lax.all_to_all(send, everyone, split_axis=0, concat_axis=0, tiled=True)  35.9 us
    all_to_all x1, blocking collectives, steps(): lax.all_to_all(parts, 'tp', split_axis=0, concat_axis=0, tiled=True)  25 us
    pallas_call x1, Pallas kernels, steps(): call(functools.partial(grad_kernel, float(rows * owners)), [shape((slots,...  3 us
    pallas_call x1, Pallas kernels, steps(): call(functools.partial(partial_kernel, cap), [shape((slots, columns), f32...  2.79 us
    pallas_call x1, Pallas kernels, steps(): call(functools.partial(send_kernel, cap), [shape((owners, deep, LANES), b...  2.78 us

profile of v4, /device:TPU:1, one launch (start us, length us, event | category | flops | bytes accessed | tf_op | source)
XLA Modules:
  0.0 70.1 jit_solution(679264144771592035)
XLA Ops:
  0.6 2.8 %shard_map.95 = bf16[32,232,128]{2,1,0:T(8,128)(2,1)S(1)} custom-call(s32[128]{0:T(128)} %ids_hbm.1, bf16[128]{0:T(256)(128)(2,1)} %old_hbm.1, s32[128]{0:T(128)} %owner_hbm.1, s32[2]{0:T(128)} %len_hbm.1, bf16[128,4864]{1,0:T(8,128)(2,1)} %ref_hbm.1), custom_call_target="tpu_custom_call" | custom-call | tf_op jit(solution)/shard_map/pallas_call | solution.py:364
  3.4 0.0 copy-start
  3.4 35.9 %all_to_all.10.got_ref = bf16[32,232,128]{2,1,0:T(8,128)(2,1)S(1)} all-to-all(bf16[32,232,128]{2,1,0:T(8,128)(2,1)S(1)} %shard_map.95), channel_id=1, replica_groups=mesh['role'=4,'dp'=8,'tp'=16] {'role','dp'}, dimensions={0} | all-to-all | bytes 3801088 | tf_op jit(solution)/shard_map/all_to_all | solution.py:380
  39.3 0.0 copy-done
  39.3 0.0 copy-start.1
  39.3 0.0 copy-start.2
  39.3 2.8 %shard_map.96 = (f32[192,4864]{1,0:T(8,128)S(1)}, f32[192,4864]{1,0:T(8,128)S(1)}, f32[16,2,384]{2,1,0:T(2,128)S(1)}, f32[8,256]{1,0:T(8,128)S(1)}) custom-call(bf16[32,232,128]{2,1,0:T(8,128)(2,1)S(1)} %all_to_all.10.got_ref, bf16[192,4864]{1,0:T(8,128)(2,1)S(1)} %copy-done), custom_call_target="tpu_custom_call" | custom-call | tf_op jit(solution)/shard_map/pallas_call | solution.py:381
  42.1 25.0 %all_to_all.11.all_ref = f32[16,2,384]{2,1,0:T(2,128)S(1)} all-to-all(f32[16,2,384]{2,1,0:T(2,128)S(1)} %get-tuple-element.6), channel_id=1, replica_groups=mesh['role'=4,'dp'=8,'tp'=16] {'tp'}, dimensions={0} | all-to-all | bytes 98304 | tf_op jit(solution)/shard_map/all_to_all | solution.py:393
  67.1 0.0 copy-done.1
  67.1 0.0 copy-done.2
  67.1 3.0 %shard_map.97 = (bf16[192,4864]{1,0:T(8,128)(2,1)}, f32[192]{0:T(256)}) custom-call(f32[16,2,384]{2,1,0:T(2,128)S(1)} %all_to_all.11.all_ref, f32[8,256]{1,0:T(8,128)S(1)} %get-tuple-element.7.meta_ref, f32[64]{0:T(128)S(1)} %copy-done.1, s32[64]{0:T(128)S(1)} %copy-done.2, f32[192,4864]{1,0:T(8,128)S(1)} %get-tuple-element.8.exp_ref, ...), custom_call_target="tpu_custom_call" | custom-call | tf_op jit(solution)/shard_map/pallas_call | solution.py:395
Async XLA Ops:
  3.4 35.9 %copy-start = (bf16[192,4864]{1,0:T(8,128)(2,1)S(1)}, bf16[192,4864]{1,0:T(8,128)(2,1)}, u32[]{:S(2)}) copy-start(bf16[192,4864]{1,0:T(8,128)(2,1)} %pol_ref.1) | copy-start | bytes 5603332
  39.3 27.8 %copy-start.1 = (f32[64]{0:T(128)S(1)}, f32[64]{0:T(128)}, u32[]{:S(2)}) copy-start(f32[64]{0:T(128)} %rewards_ref.1) | copy-start | bytes 772
  39.3 27.8 %copy-start.2 = (s32[64]{0:T(128)S(1)}, s32[64]{0:T(128)}, u32[]{:S(2)}) copy-start(s32[64]{0:T(128)} %group_ref.1) | copy-start | bytes 772

commit v5 on v4

--- a/solution.py
+++ b/solution.py
@@ -81,7 +81,7 @@
         (ids >> 16).astype(f32),
         old_ref[...].reshape(1, rows).astype(f32),
         tag.astype(f32),
-        jnp.ones((1, rows), f32),
+        *(jnp.ones((1, rows), f32) for _ in range(3)),
     )
     place_of = feature - (slot & 1) * HALF
     for n, value in enumerate(values):
@@ -106,13 +106,16 @@
                 hit = mine & (place + (o * OCTET * cap - first) == slot.reshape(1, 1, rows))
                 parts.append(hit.astype(f32).reshape(OCTET * half, rows).astype(bf16))
             pickers.append(jnp.concatenate(parts, axis=1))
-    last_row = iota((OCTET, half, LANES), 1)
-    highest = None
-    tails = []
+    pickers = [jnp.concatenate(pickers[side::2], axis=0) for side in range(2)]
+    last_row = iota((owners, half, LANES), 1)
+    tops, sums = [], []
     for n, g in enumerate(range(0, full, 2)):
-        loads[n].wait()
-        for c in range(g * GROUP, min((g + 2) * GROUP, blocks)):
-            highest = block(c) if highest is None else jnp.maximum(highest, block(c))
+        for copy in loads[:1] if n == 0 else loads[1:] if n == 1 else ():
+            copy.wait()
+        here = [block(c) for c in range(g * GROUP, min((g + 2) * GROUP, blocks))]
+        tops.append(jnp.max(functools.reduce(jnp.maximum, here).astype(f32), axis=1, keepdims=True))
+        level = jnp.broadcast_to(tops[-1], (rows, LANES))
+        sums.append(jnp.sum(sum(jnp.exp(x.astype(f32) - level) for x in here), axis=1, keepdims=True))
         right = [
             jnp.concatenate(
                 [
@@ -123,27 +126,29 @@
             )
             for side in range(2)
         ]
-        for o in range(owners // OCTET):
-            out = [
-                jnp.dot(pickers[2 * o + side], right[side], preferred_element_type=f32).reshape(OCTET, half, 2 * LANES)
-                for side in range(2)
-            ]
-            both = jnp.concatenate([out[0][:, 0:8], out[0][:, 8:] + out[1][:, : half - 8], out[1][:, half - 8 :]], axis=1)
-            for h in range(min(2, full - g)):
-                send_ref[o * OCTET : (o + 1) * OCTET, (g + h) * tall : (g + h + 1) * tall, :] = both[
-                    :, :, h * LANES : (h + 1) * LANES
-                ].astype(bf16)
-            if g + 2 > full:
-                tails.append(out[0][:, :, LANES:])
-    top = jnp.max(highest.astype(f32), axis=1, keepdims=True)
-    table = jnp.where(column == len(values) - 1, table * top, table).astype(bf16)
-    for o in range(owners // OCTET):
-        pair = iota((OCTET, half, rows), 0) * (cap // 2) + row + (o * OCTET * (cap // 2) - 2 * cap)
-        hit = (row >= 2 * cap) & (row < half - 1) & (pair == (slot >> 1).reshape(1, 1, rows))
-        picker = hit.astype(f32).reshape(OCTET * half, rows).astype(bf16)
-        extra = jnp.dot(picker, table, preferred_element_type=f32).reshape(OCTET, half, LANES)
-        tail = jnp.where(last_row == half - 1, count.astype(f32), tails[o] + extra)
-        send_ref[o * OCTET : (o + 1) * OCTET, full * tall :, :] = tail.astype(bf16)
+        out = [
+            jnp.dot(pickers[side], right[side], preferred_element_type=f32).reshape(owners, half, 2 * LANES)
+            for side in range(2)
+        ]
+        both = jnp.concatenate([out[0][:, 0:8], out[0][:, 8:] + out[1][:, : half - 8], out[1][:, half - 8 :]], axis=1)
+        for h in range(min(2, full - g)):
+            send_ref[:, (g + h) * tall : (g + h + 1) * tall, :] = both[:, :, h * LANES : (h + 1) * LANES].astype(bf16)
+        if g + 2 > full:
+            tail = out[0][:, :, LANES:]
+    top = functools.reduce(jnp.maximum, tops)
+    rest = top + jnp.log(sum(x * jnp.exp(t - top) for x, t in zip(sums, tops)))
+    for n in range(len(values) - 3, len(values)):
+        part = rest.astype(bf16).astype(f32)
+        table = jnp.where(column == n, table * part, table)
+        rest = rest - part
+    table = table.astype(bf16)
+    wide_row = iota((owners, half, rows), 1)
+    pair = iota((owners, half, rows), 0) * (cap // 2) + wide_row - 2 * cap
+    hit = (wide_row >= 2 * cap) & (wide_row < half - 1) & (pair == (slot >> 1).reshape(1, 1, rows))
+    picker = hit.astype(f32).reshape(owners * half, rows).astype(bf16)
+    extra = jnp.dot(picker, table, preferred_element_type=f32).reshape(owners, half, LANES)
+    tail = jnp.where(last_row == half - 1, count.astype(f32), tail + extra)
+    send_ref[:, full * tall :, :] = tail.astype(bf16)
 
 
 def partial_kernel(cap, got_ref, pol_ref, exp_ref, gap_ref, part_ref, meta_ref, column_ref):
@@ -204,9 +209,7 @@
         counts = counts + jnp.sum(last[:, half - 9, :], axis=0, keepdims=True)
         column = (info[:, 0:1] + 256.0 * info[:, 1:2] + 65536.0 * info[:, 2:3]).astype(i32) - base
         token = jnp.broadcast_to(column, (wide, LANES)) - lane
-        top = info[:, 5:6]
-        tops = jnp.broadcast_to(top, (wide, LANES))
-        total, cross, picked, total_q = (jnp.zeros((wide, LANES), f32) for _ in range(4))
+        total, cross, picked = (jnp.zeros((wide, LANES), f32) for _ in range(3))
         for g in range(full - 1, -1, -2):
             ways = 2 if g else 1
             product = arrived((g - ways + 1) * tall, tall, ways, order)
@@ -228,15 +231,13 @@
                 gap_ref[at, span] = gaps
                 total = total + exps
                 cross = cross + gaps
-                total_q = total_q + jnp.exp(q - tops)
                 picked = jnp.where(token == c * LANES, z, picked)
         sums = (
             peak,
             jnp.sum(total, axis=1, keepdims=True),
             jnp.sum(cross, axis=1, keepdims=True),
             jnp.sum(picked, axis=1, keepdims=True),
-            top,
-            jnp.sum(total_q, axis=1, keepdims=True),
+            info[:, 5:6] + info[:, 6:7] + info[:, 7:8],
             info[:, 3:4],
             info[:, 4:5],
             column.astype(f32),
@@ -247,13 +248,13 @@
         column_ref[at, :] = out
     column_ref[slots:, :] = jnp.ones((column_ref.shape[0] - slots, LANES), f32)
     turned = column_ref[...].T
-    peak, total, cross, picked, top, total_q = (turned[n : n + 1, :] for n in range(6))
-    pairs = ((peak + jnp.log(total), cross / total), (picked, top + jnp.log(total_q)))
+    peak, total, cross, picked, log_q = (turned[n : n + 1, :] for n in range(5))
+    pairs = ((peak + jnp.log(total), cross / total), (picked, log_q))
     for n, pair in enumerate(pairs):
         line = jnp.concatenate([value[:, :slots] for value in pair], axis=1)
         part_ref[:, n : n + 1, :] = jnp.broadcast_to(line[None], (part_ref.shape[0],) + line.shape)
     for n in range(3):
-        meta_ref[n : n + 1, :] = turned[6 + n : 7 + n, :]
+        meta_ref[n : n + 1, :] = turned[5 + n : 6 + n, :]
     meta_ref[3:4, :] = jnp.concatenate([counts] * (meta_ref.shape[1] // LANES), axis=1)
     meta_ref[4:5, :] = peak
 

time: 70.3 us -> 69.6 us (0.990)
  no operation moved by 1% of the time
where the time goes in v5:
time: 69.6 us; the launch traced here: 69.4 us
  blocking collectives  60.9 us (88%)
  Pallas kernels  7.87 us (11%)
    all_to_all x1, blocking collectives, steps(): lax.all_to_all(send, everyone, split_axis=0, concat_axis=0, tiled=True)  35.9 us
    all_to_all x1, blocking collectives, steps(): lax.all_to_all(parts, 'tp', split_axis=0, concat_axis=0, tiled=True)  25 us
    pallas_call x1, Pallas kernels, steps(): call(functools.partial(grad_kernel, float(rows * owners)), [shape((slots,...  3 us
    pallas_call x1, Pallas kernels, steps(): call(functools.partial(send_kernel, cap), [shape((owners, deep, LANES), b...  2.57 us
    pallas_call x1, Pallas kernels, steps(): call(functools.partial(partial_kernel, cap), [shape((slots, columns), f32...  2.3 us

profile of v5, /device:TPU:1, one launch (start us, length us, event | category | flops | bytes accessed | tf_op | source)
XLA Modules:
  0.0 69.4 jit_solution(17283157136101626970)
XLA Ops:
  0.6 2.6 %shard_map.95 = bf16[32,232,128]{2,1,0:T(8,128)(2,1)S(1)} custom-call(s32[128]{0:T(128)} %ids_hbm.1, bf16[128]{0:T(256)(128)(2,1)} %old_hbm.1, s32[128]{0:T(128)} %owner_hbm.1, s32[2]{0:T(128)} %len_hbm.1, bf16[128,4864]{1,0:T(8,128)(2,1)} %ref_hbm.1), custom_call_target="tpu_custom_call" | custom-call | tf_op jit(solution)/shard_map/pallas_call | solution.py:365
  3.2 0.0 copy-start
  3.2 35.9 %all_to_all.10.got_ref = bf16[32,232,128]{2,1,0:T(8,128)(2,1)S(1)} all-to-all(bf16[32,232,128]{2,1,0:T(8,128)(2,1)S(1)} %shard_map.95), channel_id=1, replica_groups=mesh['role'=4,'dp'=8,'tp'=16] {'role','dp'}, dimensions={0} | all-to-all | bytes 3801088 | tf_op jit(solution)/shard_map/all_to_all | solution.py:381
  39.1 0.0 copy-done
  39.1 0.0 copy-start.1
  39.1 0.0 copy-start.2
  39.1 2.3 %shard_map.96 = (f32[192,4864]{1,0:T(8,128)S(1)}, f32[192,4864]{1,0:T(8,128)S(1)}, f32[16,2,384]{2,1,0:T(2,128)S(1)}, f32[8,256]{1,0:T(8,128)S(1)}) custom-call(bf16[32,232,128]{2,1,0:T(8,128)(2,1)S(1)} %all_to_all.10.got_ref, bf16[192,4864]{1,0:T(8,128)(2,1)S(1)} %copy-done), custom_call_target="tpu_custom_call" | custom-call | tf_op jit(solution)/shard_map/pallas_call | solution.py:382
  41.4 25.0 %all_to_all.11.all_ref = f32[16,2,384]{2,1,0:T(2,128)S(1)} all-to-all(f32[16,2,384]{2,1,0:T(2,128)S(1)} %get-tuple-element.6), channel_id=1, replica_groups=mesh['role'=4,'dp'=8,'tp'=16] {'tp'}, dimensions={0} | all-to-all | bytes 98304 | tf_op jit(solution)/shard_map/all_to_all | solution.py:394
  66.4 0.0 copy-done.1
  66.4 0.0 copy-done.2
  66.4 3.0 %shard_map.97 = (bf16[192,4864]{1,0:T(8,128)(2,1)}, f32[192]{0:T(256)}) custom-call(f32[16,2,384]{2,1,0:T(2,128)S(1)} %all_to_all.11.all_ref, f32[8,256]{1,0:T(8,128)S(1)} %get-tuple-element.7.meta_ref, f32[64]{0:T(128)S(1)} %copy-done.1, s32[64]{0:T(128)S(1)} %copy-done.2, f32[192,4864]{1,0:T(8,128)S(1)} %get-tuple-element.8.exp_ref, ...), custom_call_target="tpu_custom_call" | custom-call | tf_op jit(solution)/shard_map/pallas_call | solution.py:396
Async XLA Ops:
  3.2 35.9 %copy-start = (bf16[192,4864]{1,0:T(8,128)(2,1)S(1)}, bf16[192,4864]{1,0:T(8,128)(2,1)}, u32[]{:S(2)}) copy-start(bf16[192,4864]{1,0:T(8,128)(2,1)} %pol_ref.1) | copy-start | bytes 5603332
  39.1 27.3 %copy-start.1 = (f32[64]{0:T(128)S(1)}, f32[64]{0:T(128)}, u32[]{:S(2)}) copy-start(f32[64]{0:T(128)} %rewards_ref.1) | copy-start | bytes 772
  39.1 27.3 %copy-start.2 = (s32[64]{0:T(128)S(1)}, s32[64]{0:T(128)}, u32[]{:S(2)}) copy-start(s32[64]{0:T(128)} %group_ref.1) | copy-start | bytes 772

commit v6 on v5

--- a/solution.py
+++ b/solution.py
@@ -112,10 +112,11 @@
     for n, g in enumerate(range(0, full, 2)):
         for copy in loads[:1] if n == 0 else loads[1:] if n == 1 else ():
             copy.wait()
-        here = [block(c) for c in range(g * GROUP, min((g + 2) * GROUP, blocks))]
-        tops.append(jnp.max(functools.reduce(jnp.maximum, here).astype(f32), axis=1, keepdims=True))
-        level = jnp.broadcast_to(tops[-1], (rows, LANES))
-        sums.append(jnp.sum(sum(jnp.exp(x.astype(f32) - level) for x in here), axis=1, keepdims=True))
+        if n < 2:
+            here = [block(c) for c in range(0, 2 * GROUP) if c < blocks] if n == 0 else [block(c) for c in range(2 * GROUP, blocks)]
+            tops.append(jnp.max(functools.reduce(jnp.maximum, here).astype(f32), axis=1, keepdims=True))
+            level = jnp.broadcast_to(tops[-1], (rows, LANES))
+            sums.append(jnp.sum(sum(jnp.exp(x.astype(f32) - level) for x in here), axis=1, keepdims=True))
         right = [
             jnp.concatenate(
                 [

time: 69.6 us -> 69.5 us (level)
  no operation moved by 1% of the time
where the time goes in v6:
time: 69.5 us; the launch traced here: 69.3 us
  blocking collectives  60.9 us (88%)
  Pallas kernels  7.7 us (11%)
    all_to_all x1, blocking collectives, steps(): lax.all_to_all(send, everyone, split_axis=0, concat_axis=0, tiled=True)  35.9 us
    all_to_all x1, blocking collectives, steps(): lax.all_to_all(parts, 'tp', split_axis=0, concat_axis=0, tiled=True)  25 us
    pallas_call x1, Pallas kernels, steps(): call(functools.partial(grad_kernel, float(rows * owners)), [shape((slots,...  3 us
    pallas_call x1, Pallas kernels, steps(): call(functools.partial(send_kernel, cap), [shape((owners, deep, LANES), b...  2.4 us
    pallas_call x1, Pallas kernels, steps(): call(functools.partial(partial_kernel, cap), [shape((slots, columns), f32...  2.3 us

profile of v6, /device:TPU:1, one launch (start us, length us, event | category | flops | bytes accessed | tf_op | source)
XLA Modules:
  0.0 69.3 jit_solution(17076323527479806800)
XLA Ops:
  0.6 2.4 %shard_map.95 = bf16[32,232,128]{2,1,0:T(8,128)(2,1)S(1)} custom-call(s32[128]{0:T(128)} %ids_hbm.1, bf16[128]{0:T(256)(128)(2,1)} %old_hbm.1, s32[128]{0:T(128)} %owner_hbm.1, s32[2]{0:T(128)} %len_hbm.1, bf16[128,4864]{1,0:T(8,128)(2,1)} %ref_hbm.1), custom_call_target="tpu_custom_call" | custom-call | tf_op jit(solution)/shard_map/pallas_call | solution.py:366
  3.0 0.0 copy-start
  3.0 35.9 %all_to_all.10.got_ref = bf16[32,232,128]{2,1,0:T(8,128)(2,1)S(1)} all-to-all(bf16[32,232,128]{2,1,0:T(8,128)(2,1)S(1)} %shard_map.95), channel_id=1, replica_groups=mesh['role'=4,'dp'=8,'tp'=16] {'role','dp'}, dimensions={0} | all-to-all | bytes 3801088 | tf_op jit(solution)/shard_map/all_to_all | solution.py:382
  38.9 0.0 copy-done
  38.9 0.0 copy-start.1
  38.9 0.0 copy-start.2
  38.9 2.3 %shard_map.96 = (f32[192,4864]{1,0:T(8,128)S(1)}, f32[192,4864]{1,0:T(8,128)S(1)}, f32[16,2,384]{2,1,0:T(2,128)S(1)}, f32[8,256]{1,0:T(8,128)S(1)}) custom-call(bf16[32,232,128]{2,1,0:T(8,128)(2,1)S(1)} %all_to_all.10.got_ref, bf16[192,4864]{1,0:T(8,128)(2,1)S(1)} %copy-done), custom_call_target="tpu_custom_call" | custom-call | tf_op jit(solution)/shard_map/pallas_call | solution.py:383
  41.2 25.0 %all_to_all.11.all_ref = f32[16,2,384]{2,1,0:T(2,128)S(1)} all-to-all(f32[16,2,384]{2,1,0:T(2,128)S(1)} %get-tuple-element.6), channel_id=1, replica_groups=mesh['role'=4,'dp'=8,'tp'=16] {'tp'}, dimensions={0} | all-to-all | bytes 98304 | tf_op jit(solution)/shard_map/all_to_all | solution.py:395
  66.3 0.0 copy-done.1
  66.3 0.0 copy-done.2
  66.3 3.0 %shard_map.97 = (bf16[192,4864]{1,0:T(8,128)(2,1)}, f32[192]{0:T(256)}) custom-call(f32[16,2,384]{2,1,0:T(2,128)S(1)} %all_to_all.11.all_ref, f32[8,256]{1,0:T(8,128)S(1)} %get-tuple-element.7.meta_ref, f32[64]{0:T(128)S(1)} %copy-done.1, s32[64]{0:T(128)S(1)} %copy-done.2, f32[192,4864]{1,0:T(8,128)S(1)} %get-tuple-element.8.exp_ref, ...), custom_call_target="tpu_custom_call" | custom-call | tf_op jit(solution)/shard_map/pallas_call | solution.py:397
Async XLA Ops:
  3.0 35.9 %copy-start = (bf16[192,4864]{1,0:T(8,128)(2,1)S(1)}, bf16[192,4864]{1,0:T(8,128)(2,1)}, u32[]{:S(2)}) copy-start(bf16[192,4864]{1,0:T(8,128)(2,1)} %pol_ref.1) | copy-start | bytes 5603332
  38.9 27.3 %copy-start.1 = (f32[64]{0:T(128)S(1)}, f32[64]{0:T(128)}, u32[]{:S(2)}) copy-start(f32[64]{0:T(128)} %rewards_ref.1) | copy-start | bytes 772
  38.9 27.3 %copy-start.2 = (s32[64]{0:T(128)S(1)}, s32[64]{0:T(128)}, u32[]{:S(2)}) copy-start(s32[64]{0:T(128)} %group_ref.1) | copy-start | bytes 772

commit v7 on v6

--- a/solution.py
+++ b/solution.py
@@ -48,8 +48,8 @@
         )
     ]
     loads = []
-    for n, g in enumerate(range(0, full, 2)):
-        part = slice(g * GROUP * LANES, min((g + 2) * GROUP, blocks) * LANES)
+    first = min(2 * GROUP, blocks) * LANES
+    for n, part in enumerate((slice(0, first), slice(first, blocks * LANES))[: 1 + (blocks > 2 * GROUP)]):
         loads.append(pltpu.make_async_copy(ref_hbm.at[:, part], ref_ref.at[:, part], load.at[n]))
     for copy in smalls + loads:
         copy.start()
@@ -375,7 +375,7 @@
             pltpu.SMEM(lengths.shape, i32),
             vmem((rows, columns), bf16),
             sems(4),
-            sems(full // 2 + 1),
+            sems(2),
         ),
         limit=VMEM_LIMIT,
     )(*(pltpu.with_memory_space_constraint(x, pltpu.HBM) for x in (token_ids, old_logp, owner_of_row, lengths, ref_logits)))

time: 69.5 us -> 69.4 us (level)
  no operation moved by 1% of the time
where the time goes in v7:
time: 69.4 us; the launch traced here: 69.2 us
  blocking collectives  60.9 us (88%)
  Pallas kernels  7.59 us (11%)
    all_to_all x1, blocking collectives, steps(): lax.all_to_all(send, everyone, split_axis=0, concat_axis=0, tiled=True)  35.9 us
    all_to_all x1, blocking collectives, steps(): lax.all_to_all(parts, 'tp', split_axis=0, concat_axis=0, tiled=True)  25 us
    pallas_call x1, Pallas kernels, steps(): call(functools.partial(grad_kernel, float(rows * owners)), [shape((slots,...  3 us
    pallas_call x1, Pallas kernels, steps(): call(functools.partial(partial_kernel, cap), [shape((slots, columns), f32...  2.3 us
    pallas_call x1, Pallas kernels, steps(): call(functools.partial(send_kernel, cap), [shape((owners, deep, LANES), b...  2.29 us

profile of v7, /device:TPU:1, one launch (start us, length us, event | category | flops | bytes accessed | tf_op | source)
XLA Modules:
  0.0 69.2 jit_solution(10451958464242185308)
XLA Ops:
  0.6 2.3 %shard_map.95 = bf16[32,232,128]{2,1,0:T(8,128)(2,1)S(1)} custom-call(s32[128]{0:T(128)} %ids_hbm.1, bf16[128]{0:T(256)(128)(2,1)} %old_hbm.1, s32[128]{0:T(128)} %owner_hbm.1, s32[2]{0:T(128)} %len_hbm.1, bf16[128,4864]{1,0:T(8,128)(2,1)} %ref_hbm.1), custom_call_target="tpu_custom_call" | custom-call | tf_op jit(solution)/shard_map/pallas_call | solution.py:366
  2.9 0.0 copy-start
  2.9 35.9 %all_to_all.10.got_ref = bf16[32,232,128]{2,1,0:T(8,128)(2,1)S(1)} all-to-all(bf16[32,232,128]{2,1,0:T(8,128)(2,1)S(1)} %shard_map.95), channel_id=1, replica_groups=mesh['role'=4,'dp'=8,'tp'=16] {'role','dp'}, dimensions={0} | all-to-all | bytes 3801088 | tf_op jit(solution)/shard_map/all_to_all | solution.py:382
  38.8 0.0 copy-done
  38.8 0.0 copy-start.1
  38.8 0.0 copy-start.2
  38.8 2.3 %shard_map.96 = (f32[192,4864]{1,0:T(8,128)S(1)}, f32[192,4864]{1,0:T(8,128)S(1)}, f32[16,2,384]{2,1,0:T(2,128)S(1)}, f32[8,256]{1,0:T(8,128)S(1)}) custom-call(bf16[32,232,128]{2,1,0:T(8,128)(2,1)S(1)} %all_to_all.10.got_ref, bf16[192,4864]{1,0:T(8,128)(2,1)S(1)} %copy-done), custom_call_target="tpu_custom_call" | custom-call | tf_op jit(solution)/shard_map/pallas_call | solution.py:383
  41.2 25.0 %all_to_all.11.all_ref = f32[16,2,384]{2,1,0:T(2,128)S(1)} all-to-all(f32[16,2,384]{2,1,0:T(2,128)S(1)} %get-tuple-element.6), channel_id=1, replica_groups=mesh['role'=4,'dp'=8,'tp'=16] {'tp'}, dimensions={0} | all-to-all | bytes 98304 | tf_op jit(solution)/shard_map/all_to_all | solution.py:395
  66.2 0.0 copy-done.1
  66.2 0.0 copy-done.2
  66.2 3.0 %shard_map.97 = (bf16[192,4864]{1,0:T(8,128)(2,1)}, f32[192]{0:T(256)}) custom-call(f32[16,2,384]{2,1,0:T(2,128)S(1)} %all_to_all.11.all_ref, f32[8,256]{1,0:T(8,128)S(1)} %get-tuple-element.7.meta_ref, f32[64]{0:T(128)S(1)} %copy-done.1, s32[64]{0:T(128)S(1)} %copy-done.2, f32[192,4864]{1,0:T(8,128)S(1)} %get-tuple-element.8.exp_ref, ...), custom_call_target="tpu_custom_call" | custom-call | tf_op jit(solution)/shard_map/pallas_call | solution.py:397
Async XLA Ops:
  2.9 35.9 %copy-start = (bf16[192,4864]{1,0:T(8,128)(2,1)S(1)}, bf16[192,4864]{1,0:T(8,128)(2,1)}, u32[]{:S(2)}) copy-start(bf16[192,4864]{1,0:T(8,128)(2,1)} %pol_ref.1) | copy-start | bytes 5603332
  38.8 27.3 %copy-start.1 = (f32[64]{0:T(128)S(1)}, f32[64]{0:T(128)}, u32[]{:S(2)}) copy-start(f32[64]{0:T(128)} %rewards_ref.1) | copy-start | bytes 772
  38.8 27.3 %copy-start.2 = (s32[64]{0:T(128)S(1)}, s32[64]{0:T(128)}, u32[]{:S(2)}) copy-start(s32[64]{0:T(128)} %group_ref.1) | copy-start | bytes 772
